TPU v7x, 256 devices: a whole 4x4x8 slice. The times are simulated.
256 devices in a mesh: blk: 32 (over z, x_hi, core), shell: 8 (over x_lo, y).
Axes of the slice: x: 4 (x_hi: 2, x_lo: 2; x = x_hi * 2 + x_lo), y: 4, z: 8, core: 2. Of those that a mesh axis runs over, the one named last changes fastest.
Arguments:
- spectra: bfloat16 [128, 8, 256, 2048], P(None, None, 'shell', 'blk'), may hold values from -6 to 6
- selection: float32 [256, 2048], P('shell', 'blk'), may hold values from 0.3 to 3
- legendre: bfloat16 [64, 2048, 1024], P('blk'), may hold values from -0.125 to 0.125
- bessel: bfloat16 [1024, 128, 256], P(('blk', 'shell')), may hold values from -0.375 to 0.375
- order_perm: int32 [64], replicated, may hold values from 0 to 63, each once
Outputs:
- coeffs: float32 [1024, 8, 128, 128], P(('blk', 'shell'))
Inputs may be any that keep to these rules, and one draw needn't show every extreme that they name: `order_perm`: each order slot holds a different order.
All inputs are finite; a program needn't handle non-finite values.
Results may differ from a plain program's by a relative error of at most 0.0041.
Values may be sent and summed in bfloat16 or wider, within the bound.
No kernel may reach another device: no remote copies, remote signals or barrier semaphores. Data moves between devices by JAX's collectives and lax.ppermute only.
A program may use at most 128 MiB of HBM per device.

v0:
```python
import jax
import jax.numpy as jnp
from jax import lax
from jax.sharding import PartitionSpec as P


def on_device(spectra, selection, legendre, bessel, order_perm):
    blk_count = lax.axis_size("blk")
    shell_count = lax.axis_size("shell")
    column_index = (2 * order_perm[:, None] + jnp.arange(2, dtype=jnp.int32)[None, :]).reshape(-1)
    picked = jnp.take(spectra, column_index, axis=0)
    weighted = (picked.astype(jnp.float32) * selection[None, None, :, :]).astype(jnp.bfloat16)
    field_count = weighted.shape[1]
    shell_local = weighted.shape[2]
    cycle_local = weighted.shape[3]
    orders_here = legendre.shape[0]
    degree_count = legendre.shape[2]
    flat_rows = weighted.reshape(
        blk_count, 2 * orders_here, field_count * shell_local * cycle_local
    )
    arrived = lax.all_to_all(flat_rows, "blk", split_axis=0, concat_axis=0, tiled=True)
    by_order = arrived.reshape(blk_count, orders_here, 2, field_count, shell_local, cycle_local)
    table = legendre.reshape(orders_here, blk_count, cycle_local, degree_count)
    harmonic = jnp.einsum("bocfsj,objl->lfocs", by_order, table, preferred_element_type=jnp.float32)
    degree_local = degree_count // (blk_count * shell_count)
    harmonic = harmonic.astype(jnp.bfloat16).reshape(
        blk_count, shell_count, degree_local, field_count * 2 * orders_here * shell_local
    )
    regrouped = lax.all_to_all(
        lax.all_to_all(harmonic, "blk", split_axis=0, concat_axis=0, tiled=True),
        "shell",
        split_axis=1,
        concat_axis=1,
        tiled=True,
    )
    blocks = regrouped.reshape(
        blk_count, shell_count, degree_local, field_count, 2 * orders_here, shell_local
    )
    radial = bessel.reshape(degree_local, bessel.shape[1], shell_count, shell_local)
    result = jnp.einsum("bqlfxs,lkqs->lfbxk", blocks, radial, preferred_element_type=jnp.float32)
    return result.reshape(degree_local, field_count, blk_count * 2 * orders_here, bessel.shape[1])


def solution(mesh):
    in_specs = (
        P(None, None, "shell", "blk"),
        P("shell", "blk"),
        P("blk", None, None),
        P(("blk", "shell"), None, None),
        P(),
    )
    out_specs = P(("blk", "shell"), None, None, None)
    return jax.shard_map(
        on_device, mesh=mesh, in_specs=in_specs, out_specs=out_specs, check_vma=False
    )
```

profile of v0, /device:TPU:1, one launch (start us, length us, event | category | flops | bytes accessed | tf_op | source)
XLA Modules:
  0.0 311.7 jit_solution(15366724467712563353)
XLA Ops:
  0.0 0.7 broadcast_multiply_fusion
  0.7 0.1 iota_add_fusion
  0.7 0.1 add.61
  0.8 0.1 add.72
  1.0 12.9 %copy.36 = bf16[128,8,32,64]{3,2,1,0:T(8,128)(2,1)} copy(bf16[128,8,32,64]{0,3,2,1:T(8,128)(2,1)} %param.5) | data formatting | bytes 8388608 | tf_op args[0]
  13.9 10.0 %gather_fusion = bf16[128,8,32,64]{3,2,1,0:T(8,128)(2,1)} fusion(bf16[128,8,32,64]{3,2,1,0:T(8,128)(2,1)} %copy.36, s32[1024]{0:T(1024)S(1)} %pad_clamp_fusion), kind=kCustom, calls=%fused_computation | custom fusion | bytes 8389120 | tf_op jit(solution)/shard_map/jit(_take)/gather | solution.py:11
  23.8 0.0 copy-start.1
  23.8 12.6 %gather.7 = bf16[32,4,16384]{2,1,0:T(4,128)(2,1)} reshape(bf16[128,8,32,64]{3,2,1,0:T(8,128)(2,1)} %gather_fusion) | data formatting | bytes 8388608 | tf_op jit(solution)/shard_map/jit(_take)/gather | solution.py:11
  36.5 0.1 copy.33
  36.5 0.1 add.65
  36.6 0.1 copy.34
  36.7 0.1 copy.35
  36.8 0.0 copy-done.1
  36.8 0.1 mul.23
  36.9 4.9 %multiply_convert_fusion = bf16[32,4,16384]{2,1,0:T(4,128)(2,1)S(1)} fusion(f32[16384]{0:T(1024)S(1)} %mul.23, bf16[32,4,16384]{2,1,0:T(4,128)(2,1)} %gather.7, pred[32,4]{1,0:T(8,128)(4,1)S(1)} %copy.35), kind=kLoop, calls=%fused_computation.3 | loop fusion | flops 8388608 | bytes 8454272 | tf_op jit(solution)/shard_map/convert_element_type | solution.py:12
  41.8 107.7 %all_to_all.15 = bf16[32,4,16384]{2,1,0:T(4,128)(2,1)} all-to-all(bf16[32,4,16384]{2,1,0:T(4,128)(2,1)S(1)} %multiply_convert_fusion), channel_id=1, replica_groups=mesh['blk'=32,'shell'=8] {'blk'}, dimensions={0} | all-to-all | bytes 8388608 | tf_op jit(solution)/shard_map/all_to_all | solution.py:21
  149.5 12.5 %reshape.85 = bf16[32,2,2,8,32,64]{5,4,3,2,1,0:T(8,128)(2,1)} reshape(bf16[32,4,16384]{2,1,0:T(4,128)(2,1)} %all_to_all.15) | data formatting | bytes 8388608 | tf_op jit(solution)/shard_map/reshape | solution.py:22
  162.0 9.5 %fusion.6 = bf16[1024,8,2,2,32]{0,4,1,3,2:T(8,128)(2,1)S(1)} fusion(bf16[2,32,64,1024,1,1]{3,2,1,5,4,0:T(8,128)(2,1)} %bitcast.35, bf16[32,2,2,8,32,64]{5,4,3,2,1,0:T(8,128)(2,1)} %reshape.85), kind=kOutput, calls=%fused_computation.7 | convolution fusion | flops 4296015872 | bytes 14680064 | tf_op jit(solution)/shard_map/bocfsj,objl->lfocs/dot_general | solution.py:24
  171.5 15.0 %copy.39 = bf16[1024,8,2,2,32]{4,3,2,1,0:T(2,128)(2,1)} copy(bf16[1024,8,2,2,32]{0,4,1,3,2:T(8,128)(2,1)S(1)} %fusion.6) | data formatting | bytes 4194304 | tf_op jit(solution)/shard_map/convert_element_type | solution.py:26
  186.5 17.2 %reshape.69 = bf16[32,8,4,1024]{3,2,1,0:T(4,128)(2,1)S(1)} reshape(bf16[1024,8,2,2,32]{4,3,2,1,0:T(2,128)(2,1)} %copy.39) | data formatting | bytes 4194304 | tf_op jit(solution)/shard_map/reshape | solution.py:26
  203.7 0.0 copy-start
  203.7 56.5 %all_to_all.16 = bf16[32,8,4,1024]{3,2,1,0:T(4,128)(2,1)S(1)} all-to-all(bf16[32,8,4,1024]{3,2,1,0:T(4,128)(2,1)S(1)} %reshape.69), channel_id=1, replica_groups=mesh['blk'=32,'shell'=8] {'blk'}, dimensions={0} | all-to-all | bytes 4194304 | tf_op jit(solution)/shard_map/all_to_all | solution.py:30
  260.2 2.2 copy.40
  262.4 4.2 %all-to-all-start.2 = ((bf16[32,8,4,1024]{3,2,0,1:T(4,128)(2,1)}), bf16[32,8,4,1024]{3,2,0,1:T(4,128)(2,1)S(1)}, u32[]{:S(2)}, u32[]{:S(2)}) async-start(bf16[32,8,4,1024]{3,2,0,1:T(4,128)(2,1)} %copy.40), calls=%async_computation.2 | async-start | bytes 4194304 | tf_op jit(solution)/shard_map/all_to_all | solution.py:29
  266.6 0.0 copy-done
  266.6 0.2 copy.42
  266.8 26.0 %all-to-all-done.2 = bf16[32,8,4,1024]{3,2,0,1:T(4,128)(2,1)S(1)} async-done(((bf16[32,8,4,1024]{3,2,0,1:T(4,128)(2,1)}), bf16[32,8,4,1024]{3,2,0,1:T(4,128)(2,1)S(1)}, u32[]{:S(2)}, u32[]{:S(2)}) %all-to-all-start.2) | async-done | bytes 2097184 | tf_op jit(solution)/shard_map/all_to_all | solution.py:29
  292.8 6.9 %reshape.86 = bf16[32,8,4,8,4,32]{5,4,3,2,0,1:T(4,128)(2,1)} reshape(bf16[32,8,4,1024]{3,2,0,1:T(4,128)(2,1)S(1)} %all-to-all-done.2) | data formatting | bytes 4194304 | tf_op jit(solution)/shard_map/reshape | solution.py:36
  299.7 10.1 %fusion.9 = f32[4,8,32,4,128]{4,3,1,2,0:T(4,128)S(1)} fusion(bf16[4,128,8,32,1,1]{1,3,2,5,4,0:T(8,128)(2,1)S(1)} %bitcast.33, bf16[32,8,4,8,4,32]{5,4,3,2,0,1:T(4,128)(2,1)} %reshape.86), kind=kOutput, calls=%fused_computation.8 | convolution fusion | flops 268435456 | bytes 4456448 | tf_op jit(solution)/shard_map/bqlfxs,lkqs->lfbxk/dot_general | solution.py:40
  309.8 0.2 copy.44
  310.0 1.7 copy.45
  (6 shorter events, 0.0 us)
Async XLA Ops:
  23.8 13.0 %copy-start.1 = (f32[32,64]{1,0:T(8,128)S(1)}, f32[32,64]{1,0:T(8,128)}, u32[]{:S(2)}) copy-start(f32[32,64]{1,0:T(8,128)} %param.6) | copy-start | bytes 24580
  203.7 63.0 %copy-start = (bf16[4,128,256]{2,1,0:T(8,128)(2,1)S(1)}, bf16[4,128,256]{2,1,0:T(8,128)(2,1)}, u32[]{:S(2)}) copy-start(bf16[4,128,256]{2,1,0:T(8,128)(2,1)} %param.8) | copy-start | bytes 786436
  262.4 30.4 %all-to-all-start.2 = ((bf16[32,8,4,1024]{3,2,0,1:T(4,128)(2,1)}), bf16[32,8,4,1024]{3,2,0,1:T(4,128)(2,1)S(1)}, u32[]{:S(2)}, u32[]{:S(2)}) async-start(bf16[32,8,4,1024]{3,2,0,1:T(4,128)(2,1)} %copy.40), calls=%async_computation.2 | async-start | bytes 4194304 | tf_op jit(solution)/shard_map/all_to_all | solution.py:29
where the time goes:
time: 313 us; the launch traced here: 312 us
  blocking collectives  164 us (52%)
  local copies, waits for them, and re-layouts  91.9 us (29%)
  waiting for transfers between devices  26 us (8%)
  matrix products  19.6 us (6%)
  other arithmetic  5.61 us (2%)
  starting transfers between devices  4.22 us (1%)
    all_to_all x1, blocking collectives, on_device(): lax.all_to_all(flat_rows, 'blk', split_axis=0, concat_axis=0, tiled=True)  108 us
    all_to_all x1, blocking collectives, on_device(): lax.all_to_all(harmonic, 'blk', split_axis=0, concat_axis=0, tiled=True)  56.5 us
    all_to_all x1, waiting for transfers between devices, on_device(): lax.all_to_all(lax.all_to_all(harmonic, 'blk', split_axis=0, concat_axis=...  26 us
    gather x2, local copies, waits for them, and re-layouts, on_device(): picked = jnp.take(spectra, column_index, axis=0)  22.6 us
    reshape x1, local copies, waits for them, and re-layouts, on_device(): harmonic.astype(jnp.bfloat16)  17.2 us
    convert_element_type x1, local copies, waits for them, and re-layouts, on_device(): harmonic.astype(jnp.bfloat16)  15 us
    unnamed x6, local copies, waits for them, and re-layouts  13 us
    reshape x1, local copies, waits for them, and re-layouts, on_device(): arrived.reshape(blk_count, orders_here, 2, field_count, shell_local, cycl...  12.5 us
  transfers between devices with their start and end apart: 1, of which 1 were waited for; matrix products, arithmetic and copies ran while one was open for 0% of the time, Pallas kernels for 0%

commit v1 on v0

v1 whole, which is shorter than its diff:
```python
import functools
import jax
import jax.numpy as jnp
from jax import lax
from jax.experimental import pallas as pl
from jax.experimental.pallas import tpu as pltpu
from jax.sharding import PartitionSpec as P

NT = (((1,), (1,)), ((), ()))
NN = (((1,), (0,)), ((), ()))


def weigh_kernel(perm_ref, sel_ref, x_ref, o_ref, scr):
    slot = lax.broadcasted_iota(jnp.int32, (128, 64), 0) // 2
    lane = lax.broadcasted_iota(jnp.int32, (128, 64), 1)
    held = jnp.sum(jnp.where(slot == lane, perm_ref[...], 0), axis=1, keepdims=True)
    row = lax.broadcasted_iota(jnp.int32, (128, 128), 0)
    col = lax.broadcasted_iota(jnp.int32, (128, 128), 1)
    pick = jnp.where(2 * held + row % 2 == col, 1.0, 0.0).astype(jnp.bfloat16)
    for g in range(8):
        y = lax.dot_general(
            pick, x_ref[0, g * 256 : (g + 1) * 256, :], NT, preferred_element_type=jnp.float32
        )
        for h in range(2):
            rp = 2 * g + h
            scr[pl.ds(rp, 128, stride=16), :] = y[:, h * 128 : (h + 1) * 128] * sel_ref[rp : rp + 1, :]
    o_ref[:, 0, :, :] = scr[...].reshape(128, 16, 128).astype(jnp.bfloat16)


def weigh(perm, sel, x, half):
    return pl.pallas_call(
        weigh_kernel,
        grid=(4,),
        in_specs=[
            pl.BlockSpec((1, 64), lambda i: (0, 0)),
            pl.BlockSpec((16, 128), lambda i: (0, 0)),
            pl.BlockSpec((1, 2048, 128), lambda i: (4 * half + i, 0, 0)),
        ],
        out_specs=pl.BlockSpec((128, 1, 16, 128), lambda i: (0, i, 0, 0)),
        out_shape=jax.ShapeDtypeStruct((128, 4, 16, 128), jnp.bfloat16),
        scratch_shapes=[pltpu.VMEM((2048, 128), jnp.float32)],
        name="weigh",
        cost_estimate=pl.CostEstimate(flops=2 * 8192 * 128 * 128, bytes_accessed=4 << 20, transcendentals=0),
    )(perm, sel, x)


LT = 256


def angular_kernel(r_ref, leg_ref, o_ref, lhs, scr):
    @pl.when(pl.program_id(0) == 0)
    def _():
        for p in range(4):
            s, c = p // 2, p % 2
            for g in range(16):
                a = r_ref[2 * g, p * 64 : (p + 1) * 64, :]
                b = r_ref[2 * g + 1, p * 64 : (p + 1) * 64, :]
                ks = slice(g * 128, (g + 1) * 128)
                lhs[s, c * 128 : c * 128 + 64, ks] = jnp.concatenate([a[:, :64], b[:, :64]], axis=1)
                lhs[s, c * 128 + 64 : c * 128 + 128, ks] = jnp.concatenate([a[:, 64:], b[:, 64:]], axis=1)

    for s in range(2):
        h = lax.dot_general(lhs[s], leg_ref[s], NN, preferred_element_type=jnp.float32)
        ht = h.T
        for c in range(2):
            scr[pl.ds(2 * s + c, LT, stride=4), :] = ht[:, c * 128 : (c + 1) * 128]
    o_ref[...] = scr[...].astype(jnp.bfloat16)


def angular(r, leg):
    return pl.pallas_call(
        angular_kernel,
        grid=(1024 // LT,),
        in_specs=[
            pl.BlockSpec(memory_space=pltpu.VMEM),
            pl.BlockSpec((2, 2048, LT), lambda i: (0, 0, i)),
        ],
        out_specs=pl.BlockSpec((LT * 4, 128), lambda i: (i, 0)),
        out_shape=jax.ShapeDtypeStruct((4096, 128), jnp.bfloat16),
        scratch_shapes=[pltpu.VMEM((2, 256, 2048), jnp.bfloat16), pltpu.VMEM((LT * 4, 128), jnp.float32)],
        name="angular",
        cost_estimate=pl.CostEstimate(flops=2 * 512 * 2048 * 1024, bytes_accessed=11 << 20, transcendentals=0),
    )(r, leg)


def radial_kernel(r_ref, bes_ref, *rest):
    o_ref, wide, spread, weight = rest[-4:]
    l = pl.program_id(0)

    @pl.when(l == 0)
    def _():
        wide[...] = r_ref[...].astype(jnp.float32)
        src = lax.broadcasted_iota(jnp.int32, (256, 1024), 0)
        lam = lax.broadcasted_iota(jnp.int32, (256, 1024), 1)
        shell = (lam // 128) * 32 + 2 * (lam % 16) + (lam // 64) % 2
        spread[...] = jnp.where(src == shell, 1.0, 0.0).astype(jnp.bfloat16)

    tiled = lax.dot_general(bes_ref[0], spread[...], NN, preferred_element_type=jnp.float32)
    field = (lax.broadcasted_iota(jnp.int32, (128, 1024), 1) // 16) % 4
    for f in range(4):
        weight[f * 128 : (f + 1) * 128, :] = jnp.where(field == f, tiled, 0.0).astype(jnp.bfloat16)
    lhs = jnp.concatenate(
        [
            jnp.concatenate([wide[pl.ds(l * 4 + q * 16 + p, 32, stride=128), :] for p in range(4)], axis=0)
            for q in range(8)
        ],
        axis=1,
    ).astype(jnp.bfloat16)
    y = lax.dot_general(lhs, weight[...], NT, preferred_element_type=jnp.float32)
    for f in range(4):
        for p in range(4):
            o_ref[0, f, pl.ds(p, 32, stride=4), :] = y[p * 32 : (p + 1) * 32, f * 128 : (f + 1) * 128]


def radial(r, bes, half, prior):
    more = () if prior is None else (prior,)
    return pl.pallas_call(
        radial_kernel,
        grid=(4,),
        in_specs=[
            pl.BlockSpec(memory_space=pltpu.VMEM),
            pl.BlockSpec((1, 128, 256), lambda i: (i, 0, 0)),
        ]
        + [pl.BlockSpec(memory_space=pl.ANY)] * len(more),
        out_specs=pl.BlockSpec((1, 4, 128, 128), lambda i: (i, half, 0, 0)),
        out_shape=jax.ShapeDtypeStruct((4, 8, 128, 128), jnp.float32),
        scratch_shapes=[
            pltpu.VMEM((4096, 128), jnp.float32),
            pltpu.VMEM((256, 1024), jnp.bfloat16),
            pltpu.VMEM((512, 1024), jnp.bfloat16),
        ],
        input_output_aliases={2: 0} if more else {},
        name="radial",
        cost_estimate=pl.CostEstimate(flops=2 * 4 * 128 * 1024 * 512, bytes_accessed=3 << 20, transcendentals=0),
    )(r, bes, *more)


def on_device(spectra, selection, legendre, bessel, order_perm):
    x = jnp.transpose(spectra, (1, 2, 3, 0)).reshape(8, 2048, 128)
    sel = selection.reshape(16, 128)
    perm = order_perm.reshape(1, 64)
    out = None
    for half in range(2):
        w = weigh(perm, sel, x, half).reshape(32, 256, 128)
        w = lax.all_to_all(w, "blk", split_axis=0, concat_axis=0, tiled=True)
        h = angular(w, legendre).reshape(256, 16, 128)
        h = lax.all_to_all(h, ("blk", "shell"), split_axis=0, concat_axis=0, tiled=True)
        out = radial(h.reshape(4096, 128), bessel, half, out)
    return out


def solution(mesh):
    in_specs = (
        P(None, None, "shell", "blk"),
        P("shell", "blk"),
        P("blk", None, None),
        P(("blk", "shell"), None, None),
        P(),
    )
    out_specs = P(("blk", "shell"), None, None, None)
    return jax.shard_map(
        on_device, mesh=mesh, in_specs=in_specs, out_specs=out_specs, check_vma=False
    )
```

time: 313 us -> 212 us (0.68)
  blocking collectives: 164 us -> 0 us
  waiting for transfers between devices: 26 us -> 136 us
  local copies, waits for them, and re-layouts: 91.9 us -> 3.68 us
  Pallas kernels: 0 us -> 36.4 us
  starting transfers between devices: 4.22 us -> 34.8 us
  matrix products: 19.6 us -> 0 us
  other arithmetic: 5.61 us -> 0 us
    all_to_all x2 -> x0, blocking collectives: 164 us -> none  [the longest x1 108 us: on_device(): lax.all_to_all(flat_rows, 'blk', split_axis=0, concat_axis=0, tiled=True)]
    all_to_all x1 -> x4, waiting for transfers between devices: 26 us -> 136 us  [the longest x2 87.2 us: on_device(): w = lax.all_to_all(w, 'blk', split_axis=0, concat_axis=0, tiled=True)]
    reshape x4 -> x1, local copies, waits for them, and re-layouts: 38.2 us -> 1.38 us  [on_device(): sel = selection.reshape(16, 128)]
    pallas_call x0 -> x6, Pallas kernels: none -> 36.4 us  [the longest x2 16.2 us: angular(): pl.pallas_call(angular_kernel, grid=(1024 // LT,), in_specs=[pl.BlockSpec...]
    all_to_all x1 -> x4, starting transfers between devices: 4.22 us -> 34.8 us  [the longest x2 19 us: on_device(): w = lax.all_to_all(w, 'blk', split_axis=0, concat_axis=0, tiled=True)]
    gather x2 -> x0, local copies, waits for them, and re-layouts: 22.6 us -> none  [on_device(): picked = jnp.take(spectra, column_index, axis=0)]
    dot_general x2 -> x0, matrix products: 19.6 us -> none  [the longest x1 10.1 us: on_device(): jnp.einsum('bqlfxs,lkqs->lfbxk', blocks, radial, preferred_element_type=j...]
    convert_element_type x1 -> x0, local copies, waits for them, and re-layouts: 15 us -> none  [on_device(): harmonic.astype(jnp.bfloat16)]
  transfers between devices with their start and end apart: 1 -> 4, of which waited for: 1 -> 4; matrix products, arithmetic and copies ran while one was open for 0% -> 0% of each run, Pallas kernels for 0% -> 12%
where the time goes in v1:
time: 212 us; the launch traced here: 211 us
  waiting for transfers between devices  136 us (64%)
  Pallas kernels  36.4 us (17%)
  starting transfers between devices  34.8 us (16%)
  local copies, waits for them, and re-layouts  3.68 us (2%)
    all_to_all x2, waiting for transfers between devices, on_device(): w = lax.all_to_all(w, 'blk', split_axis=0, concat_axis=0, tiled=True)  87.2 us
    all_to_all x2, waiting for transfers between devices, on_device(): lax.all_to_all(h, ('blk', 'shell'), split_axis=0, concat_axis=0, tiled=True)  48.8 us
    all_to_all x2, starting transfers between devices, on_device(): w = lax.all_to_all(w, 'blk', split_axis=0, concat_axis=0, tiled=True)  19 us
    pallas_call x2, Pallas kernels, angular(): pl.pallas_call(angular_kernel, grid=(1024 // LT,), in_specs=[pl.BlockSpec...  16.2 us
    all_to_all x2, starting transfers between devices, on_device(): lax.all_to_all(h, ('blk', 'shell'), split_axis=0, concat_axis=0, tiled=True)  15.8 us
    pallas_call x2, Pallas kernels, radial(): pl.pallas_call(radial_kernel, grid=(4,), in_specs=[pl.BlockSpec(memory_sp...  10.4 us
    pallas_call x2, Pallas kernels, weigh(): pl.pallas_call(weigh_kernel, grid=(4,), in_specs=[pl.BlockSpec((1, 64), l...  9.86 us
  transfers between devices with their start and end apart: 4, of which 4 were waited for; matrix products, arithmetic and copies ran while one was open for 0% of the time, Pallas kernels for 12%

profile of v1, /device:TPU:1, one launch (start us, length us, event | category | flops | bytes accessed | tf_op | source)
XLA Modules:
  0.0 211.0 jit_solution(6827485931024150587)
XLA Ops:
  0.0 1.4 reshape.28.sel_ref
  1.4 5.0 %weigh.3 = bf16[128,4,16,128]{3,2,1,0:T(8,128)(2,1)} custom-call(s32[1,64]{1,0:T(1,128)} %bitcast.18, f32[16,128]{1,0:T(8,128)} %reshape.28.sel_ref, bf16[8,2048,128]{2,1,0:T(8,128)(2,1)} %bitcast.10), custom_call_target="tpu_custom_call" | custom-call | flops 268435456 | bytes 4194304 | tf_op jit(solution)/shard_map/weigh/pallas_call | solution.py:31
  6.3 12.6 %all-to-all-start.2 = ((bf16[32,256,128]{2,1,0:T(8,128)(2,1)}), bf16[32,256,128]{2,1,0:T(8,128)(2,1)S(1)}, u32[]{:S(2)}, u32[]{:S(2)}) async-start(bf16[32,256,128]{2,1,0:T(8,128)(2,1)} %bitcast.13), calls=%async_computation.2 | async-start | bytes 4194304 | tf_op jit(solution)/shard_map/all_to_all | solution.py:145
  18.9 4.9 %weigh.2 = bf16[128,4,16,128]{3,2,1,0:T(8,128)(2,1)} custom-call(s32[1,64]{1,0:T(1,128)} %bitcast.19, f32[16,128]{1,0:T(8,128)} %reshape.28.sel_ref, bf16[8,2048,128]{2,1,0:T(8,128)(2,1)} %bitcast.11), custom_call_target="tpu_custom_call" | custom-call | flops 268435456 | bytes 4194304 | tf_op jit(solution)/shard_map/weigh/pallas_call | solution.py:31
  23.8 45.2 %all-to-all-done.2.r_ref = bf16[32,256,128]{2,1,0:T(8,128)(2,1)S(1)} async-done(((bf16[32,256,128]{2,1,0:T(8,128)(2,1)}), bf16[32,256,128]{2,1,0:T(8,128)(2,1)S(1)}, u32[]{:S(2)}, u32[]{:S(2)}) %all-to-all-start.2) | async-done | bytes 2097184 | tf_op jit(solution)/shard_map/all_to_all | solution.py:145
  69.0 0.0 copy-start
  69.0 1.3 copy-done
  70.3 6.4 %all-to-all-start = ((bf16[32,256,128]{2,1,0:T(8,128)(2,1)}), bf16[32,256,128]{2,1,0:T(8,128)(2,1)}, u32[]{:S(2)}, u32[]{:S(2)}) async-start(bf16[32,256,128]{2,1,0:T(8,128)(2,1)} %bitcast.12), calls=%async_computation | async-start | bytes 4194304 | tf_op jit(solution)/shard_map/all_to_all | solution.py:145
  76.7 8.1 %angular.3 = bf16[4096,128]{1,0:T(8,128)(2,1)} custom-call(bf16[32,256,128]{2,1,0:T(8,128)(2,1)} %copy-done, bf16[2,2048,1024]{2,1,0:T(8,128)(2,1)} %leg_ref.3), custom_call_target="tpu_custom_call" | custom-call | flops 2147483648 | bytes 11534336 | tf_op jit(solution)/shard_map/angular/pallas_call | solution.py:71
  84.9 42.0 %all-to-all-done.r_ref = bf16[32,256,128]{2,1,0:T(8,128)(2,1)} async-done(((bf16[32,256,128]{2,1,0:T(8,128)(2,1)}), bf16[32,256,128]{2,1,0:T(8,128)(2,1)}, u32[]{:S(2)}, u32[]{:S(2)}) %all-to-all-start) | async-done | bytes 2097184 | tf_op jit(solution)/shard_map/all_to_all | solution.py:145
  126.9 9.4 %all-to-all-start.3 = ((bf16[256,16,128]{2,1,0:T(8,128)(2,1)}), bf16[256,16,128]{2,1,0:T(8,128)(2,1)S(1)}, u32[]{:S(2)}, u32[]{:S(2)}) async-start(bf16[256,16,128]{2,1,0:T(8,128)(2,1)} %bitcast.16), calls=%async_computation.3 | async-start | bytes 2097152 | tf_op jit(solution)/shard_map/all_to_all | solution.py:147
  136.3 8.1 %angular.2 = bf16[4096,128]{1,0:T(8,128)(2,1)} custom-call(bf16[32,256,128]{2,1,0:T(8,128)(2,1)} %all-to-all-done.r_ref, bf16[2,2048,1024]{2,1,0:T(8,128)(2,1)} %leg_ref.3), custom_call_target="tpu_custom_call" | custom-call | flops 2147483648 | bytes 11534336 | tf_op jit(solution)/shard_map/angular/pallas_call | solution.py:71
  144.4 22.9 %all-to-all-done.3 = bf16[256,16,128]{2,1,0:T(8,128)(2,1)S(1)} async-done(((bf16[256,16,128]{2,1,0:T(8,128)(2,1)}), bf16[256,16,128]{2,1,0:T(8,128)(2,1)S(1)}, u32[]{:S(2)}, u32[]{:S(2)}) %all-to-all-start.3) | async-done | bytes 1048608 | tf_op jit(solution)/shard_map/all_to_all | solution.py:147
  167.4 0.0 copy-start.1
  167.4 6.4 %all-to-all-start.1 = ((bf16[256,16,128]{2,1,0:T(8,128)(2,1)}), bf16[256,16,128]{2,1,0:T(8,128)(2,1)S(1)}, u32[]{:S(2)}, u32[]{:S(2)}) async-start(bf16[256,16,128]{2,1,0:T(8,128)(2,1)} %bitcast.17), calls=%async_computation.1 | async-start | bytes 2097152 | tf_op jit(solution)/shard_map/all_to_all | solution.py:147
  173.8 0.0 copy-done.1
  173.8 5.2 %radial.2.rest_0_ = f32[4,8,128,128]{3,2,1,0:T(8,128)} custom-call(bf16[4096,128]{1,0:T(8,128)(2,1)} %bitcast.14, bf16[4,128,256]{2,1,0:T(8,128)(2,1)} %bes_ref.3), custom_call_target="tpu_custom_call" | custom-call | flops 536870912 | bytes 3145728 | tf_op jit(solution)/shard_map/radial/pallas_call | solution.py:117
  179.0 25.8 %all-to-all-done.1 = bf16[256,16,128]{2,1,0:T(8,128)(2,1)S(1)} async-done(((bf16[256,16,128]{2,1,0:T(8,128)(2,1)}), bf16[256,16,128]{2,1,0:T(8,128)(2,1)S(1)}, u32[]{:S(2)}, u32[]{:S(2)}) %all-to-all-start.1) | async-done | bytes 1048608 | tf_op jit(solution)/shard_map/all_to_all | solution.py:147
  204.8 0.0 copy-start.2
  204.8 1.0 copy-done.2
  205.8 5.2 %radial.3 = f32[4,8,128,128]{3,2,1,0:T(8,128)} custom-call(bf16[4096,128]{1,0:T(8,128)(2,1)} %bitcast.15, bf16[4,128,256]{2,1,0:T(8,128)(2,1)} %bes_ref.3, f32[4,8,128,128]{3,2,1,0:T(8,128)} %radial.2.rest_0_), custom_call_target="tpu_custom_call", output_to_operand_aliasing={{}: (2, {})} | custom-call | flops 536870912 | bytes 3145728 | tf_op jit(solution)/shard_map/radial/pallas_call | solution.py:117
Async XLA Ops:
  6.3 62.6 %all-to-all-start.2 = ((bf16[32,256,128]{2,1,0:T(8,128)(2,1)}), bf16[32,256,128]{2,1,0:T(8,128)(2,1)S(1)}, u32[]{:S(2)}, u32[]{:S(2)}) async-start(bf16[32,256,128]{2,1,0:T(8,128)(2,1)} %bitcast.13), calls=%async_computation.2 | async-start | bytes 4194304 | tf_op jit(solution)/shard_map/all_to_all | solution.py:145
  69.0 1.3 copy-start
  70.3 56.5 %all-to-all-start = ((bf16[32,256,128]{2,1,0:T(8,128)(2,1)}), bf16[32,256,128]{2,1,0:T(8,128)(2,1)}, u32[]{:S(2)}, u32[]{:S(2)}) async-start(bf16[32,256,128]{2,1,0:T(8,128)(2,1)} %bitcast.12), calls=%async_computation | async-start | bytes 4194304 | tf_op jit(solution)/shard_map/all_to_all | solution.py:145
  126.9 40.5 %all-to-all-start.3 = ((bf16[256,16,128]{2,1,0:T(8,128)(2,1)}), bf16[256,16,128]{2,1,0:T(8,128)(2,1)S(1)}, u32[]{:S(2)}, u32[]{:S(2)}) async-start(bf16[256,16,128]{2,1,0:T(8,128)(2,1)} %bitcast.16), calls=%async_computation.3 | async-start | bytes 2097152 | tf_op jit(solution)/shard_map/all_to_all | solution.py:147
  167.4 6.4 %copy-start.1 = (bf16[256,16,128]{2,1,0:T(8,128)(2,1)}, bf16[256,16,128]{2,1,0:T(8,128)(2,1)S(1)}, u32[]{:S(2)}) copy-start(bf16[256,16,128]{2,1,0:T(8,128)(2,1)S(1)} %all-to-all-done.3) | copy-start | bytes 3145732
  167.4 37.4 %all-to-all-start.1 = ((bf16[256,16,128]{2,1,0:T(8,128)(2,1)}), bf16[256,16,128]{2,1,0:T(8,128)(2,1)S(1)}, u32[]{:S(2)}, u32[]{:S(2)}) async-start(bf16[256,16,128]{2,1,0:T(8,128)(2,1)} %bitcast.17), calls=%async_computation.1 | async-start | bytes 2097152 | tf_op jit(solution)/shard_map/all_to_all | solution.py:147
  204.8 1.0 copy-start.2

commit v2 on v0

v2 whole, which is shorter than its diff:
```python
import functools
import jax
import jax.numpy as jnp
from jax import lax
from jax.experimental import pallas as pl
from jax.experimental.pallas import tpu as pltpu
from jax.sharding import PartitionSpec as P

NT = (((1,), (1,)), ((), ()))
NN = (((1,), (0,)), ((), ()))
BF = jnp.bfloat16
F32 = jnp.float32
WHOLE = pl.BlockSpec(memory_space=pltpu.VMEM)


def cost(flops, moved):
    return pl.CostEstimate(flops=flops, bytes_accessed=moved, transcendentals=0)


PITCH = 16


def weigh_kernel(perm_ref, sel_ref, x_ref, o_ref, scr):
    p = lax.broadcasted_iota(jnp.int32, (128, 64), 0)
    lane = lax.broadcasted_iota(jnp.int32, (128, 64), 1)
    held = jnp.sum(jnp.where(p // 2 == lane, 2 * perm_ref[...] + p % 2, 0), axis=1, keepdims=True)
    col = lax.broadcasted_iota(jnp.int32, (128, 128), 1)
    pick = jnp.where(held == col, 1.0, 0.0).astype(BF)
    for g in range(8):
        y = lax.dot_general(pick, x_ref[0, g * 256 : (g + 1) * 256, :], NT, preferred_element_type=F32)
        for h in range(2):
            rp = 2 * g + h
            scr[pl.ds(rp, 128, stride=PITCH), :] = y[:, h * 128 : (h + 1) * 128] * sel_ref[rp : rp + 1, :]
    if PITCH == 16:
        o_ref[:, 0, :, :] = scr[...].reshape(128, 16, 128).astype(BF)
    else:
        for q in range(128):
            o_ref[q, 0, :, :] = scr[q * PITCH : q * PITCH + 16, :].astype(BF)


def weigh(perm, sel, x):
    return pl.pallas_call(
        weigh_kernel,
        grid=(8,),
        in_specs=[
            pl.BlockSpec((1, 64), lambda i: (0, 0)),
            pl.BlockSpec((16, 128), lambda i: (0, 0)),
            pl.BlockSpec((1, 2048, 128), lambda i: (i, 0, 0)),
        ],
        out_specs=pl.BlockSpec((128, 1, 16, 128), lambda i: (0, i, 0, 0)),
        out_shape=jax.ShapeDtypeStruct((128, 8, 16, 128), BF),
        scratch_shapes=[pltpu.VMEM((128 * PITCH, 128), F32)],
        name="weigh",
        cost_estimate=cost(2 * 16384 * 128 * 128, 8 << 20),
    )(perm, sel, x)


LT = 256
LP = 8


def angular_kernel(r_ref, leg_ref, o_ref, lhs, scr):
    @pl.when(pl.program_id(0) == 0)
    def _():
        for p in range(4):
            s, c = p // 2, p % 2
            for fh in range(2):
                rows = slice(p * 128 + fh * 64, p * 128 + fh * 64 + 64)
                to = c * 256 + fh * 128
                for g in range(16):
                    a = r_ref[2 * g, rows, :]
                    b = r_ref[2 * g + 1, rows, :]
                    ks = slice(g * 128, (g + 1) * 128)
                    lhs[s, to : to + 64, ks] = jnp.concatenate([a[:, :64], b[:, :64]], axis=1)
                    lhs[s, to + 64 : to + 128, ks] = jnp.concatenate([a[:, 64:], b[:, 64:]], axis=1)

    for s in range(2):
        h = lax.dot_general(lhs[s], leg_ref[s], NN, preferred_element_type=F32)
        ht = h.T
        for n in range(4):
            scr[pl.ds(4 * s + n, LT, stride=LP), :] = ht[:, n * 128 : (n + 1) * 128]
    if LP == 8:
        o_ref[...] = scr[...].astype(BF)
    else:
        for l in range(0, LT, 2):
            o_ref[l * 8 : l * 8 + 16, :] = jnp.concatenate(
                [scr[l * LP : l * LP + 8, :], scr[(l + 1) * LP : (l + 1) * LP + 8, :]], axis=0
            ).astype(BF)


def angular(r, leg):
    return pl.pallas_call(
        angular_kernel,
        grid=(1024 // LT,),
        in_specs=[WHOLE, pl.BlockSpec((2, 2048, LT), lambda i: (0, 0, i))],
        out_specs=pl.BlockSpec((LT * 8, 128), lambda i: (i, 0)),
        out_shape=jax.ShapeDtypeStruct((8192, 128), BF),
        scratch_shapes=[pltpu.VMEM((2, 512, 2048), BF), pltpu.VMEM((LT * LP, 128), F32)],
        name="angular",
        cost_estimate=cost(2 * 1024 * 2048 * 1024, 14 << 20),
    )(r, leg)


def spread_kernel(bes_ref, o_ref):
    src = lax.broadcasted_iota(jnp.int32, (256, 1024), 0)
    lam = lax.broadcasted_iota(jnp.int32, (256, 1024), 1)
    shell = (lam // 128) * 32 + 2 * (lam % 16) + (lam // 64) % 2
    one = jnp.where(src == shell, 1.0, 0.0).astype(BF)
    o_ref[...] = lax.dot_general(bes_ref[...], one, NN, preferred_element_type=F32).astype(BF)


def spread(bes):
    return pl.pallas_call(
        spread_kernel,
        in_specs=[WHOLE],
        out_specs=WHOLE,
        out_shape=jax.ShapeDtypeStruct((512, 1024), BF),
        name="spread",
        cost_estimate=cost(2 * 512 * 256 * 1024, 2 << 20),
    )(bes)


def radial_kernel(r_ref, wide_ref, o_ref, f32s, weight, held):
    l = pl.program_id(0)

    @pl.when(l == 0)
    def _():
        f32s[...] = r_ref[...].astype(F32)

    field = (lax.broadcasted_iota(jnp.int32, (128, 1024), 1) // 16) % 4
    tiled = wide_ref[...]
    for f in range(4):
        weight[f * 128 : (f + 1) * 128, :] = jnp.where(field == f, tiled, jnp.zeros_like(tiled))
    for n in range(8):
        for q in range(8):
            held[n * 32 : (n + 1) * 32, q * 128 : (q + 1) * 128] = f32s[
                pl.ds(q * 32 + l * 8 + n, 32, stride=256), :
            ].astype(BF)
    y = lax.dot_general(held[...], weight[...], NT, preferred_element_type=F32)
    for n in range(8):
        p, fh = n // 2, n % 2
        for f in range(4):
            o_ref[0, fh * 4 + f, pl.ds(p, 32, stride=4), :] = y[n * 32 : (n + 1) * 32, f * 128 : (f + 1) * 128]


def radial(r, wide):
    return pl.pallas_call(
        radial_kernel,
        grid=(4,),
        in_specs=[WHOLE, pl.BlockSpec((128, 1024), lambda i: (i, 0))],
        out_specs=pl.BlockSpec((1, 8, 128, 128), lambda i: (i, 0, 0, 0)),
        out_shape=jax.ShapeDtypeStruct((4, 8, 128, 128), F32),
        scratch_shapes=[pltpu.VMEM((8192, 128), F32), pltpu.VMEM((512, 1024), BF), pltpu.VMEM((256, 1024), BF)],
        name="radial",
        cost_estimate=cost(2 * 4 * 256 * 1024 * 512, 5 << 20),
    )(r, wide)


def on_device(spectra, selection, legendre, bessel, order_perm):
    x = jnp.transpose(spectra, (1, 2, 3, 0)).reshape(8, 2048, 128)
    w = weigh(order_perm.reshape(1, 64), selection.reshape(16, 128), x).reshape(32, 512, 128)
    w = lax.all_to_all(w, "blk", split_axis=0, concat_axis=0, tiled=True)
    wide = spread(bessel.reshape(512, 256))
    h = angular(w, legendre).reshape(256, 32, 128)
    h = lax.all_to_all(h, ("blk", "shell"), split_axis=0, concat_axis=0, tiled=True)
    return radial(h.reshape(8192, 128), wide)


def solution(mesh):
    in_specs = (
        P(None, None, "shell", "blk"),
        P("shell", "blk"),
        P("blk", None, None),
        P(("blk", "shell"), None, None),
        P(),
    )
    out_specs = P(("blk", "shell"), None, None, None)
    return jax.shard_map(
        on_device, mesh=mesh, in_specs=in_specs, out_specs=out_specs, check_vma=False
    )
```

time: 313 us -> 201 us (0.64)
  local copies, waits for them, and re-layouts: 91.9 us -> 2.72 us
  blocking collectives: 164 us -> 108 us
  Pallas kernels: 0 us -> 29.5 us
  waiting for transfers between devices: 26 us -> 50.6 us
  matrix products: 19.6 us -> 0 us
  other arithmetic: 5.61 us -> 0 us
  starting transfers between devices: 4.22 us -> 8.91 us
    all_to_all x2 -> x1, blocking collectives: 164 us -> 108 us  [on_device(): w = lax.all_to_all(w, 'blk', split_axis=0, concat_axis=0, tiled=True)]
    reshape x4 -> x1, local copies, waits for them, and re-layouts: 38.2 us -> 1.38 us  [on_device(): selection.reshape(16, 128)]
    pallas_call x0 -> x4, Pallas kernels: none -> 29.5 us  [the longest x1 11.4 us: angular(): pl.pallas_call(angular_kernel, grid=(1024 // LT,), in_specs=[WHOLE, pl.Bl...]
    all_to_all x1, waiting for transfers between devices: 26 us -> 50.6 us  [on_device(): lax.all_to_all(h, ('blk', 'shell'), split_axis=0, concat_axis=0, tiled=True)]
    gather x2 -> x0, local copies, waits for them, and re-layouts: 22.6 us -> none  [on_device(): picked = jnp.take(spectra, column_index, axis=0)]
    dot_general x2 -> x0, matrix products: 19.6 us -> none  [the longest x1 10.1 us: on_device(): jnp.einsum('bqlfxs,lkqs->lfbxk', blocks, radial, preferred_element_type=j...]
    convert_element_type x1 -> x0, local copies, waits for them, and re-layouts: 15 us -> none  [on_device(): harmonic.astype(jnp.bfloat16)]
    unnamed x6 -> x2, local copies, waits for them, and re-layouts: 13 us -> 1.34 us
  transfers between devices with their start and end apart: 1 -> 1, of which waited for: 1 -> 1; matrix products, arithmetic and copies ran while one was open for 0% -> 0% of each run, Pallas kernels for 0% -> 1%
where the time goes in v2:
time: 201 us; the launch traced here: 200 us
  blocking collectives  108 us (54%)
  waiting for transfers between devices  50.6 us (25%)
  Pallas kernels  29.5 us (15%)
  starting transfers between devices  8.91 us (4%)
  local copies, waits for them, and re-layouts  2.72 us (1%)
    all_to_all x1, blocking collectives, on_device(): w = lax.all_to_all(w, 'blk', split_axis=0, concat_axis=0, tiled=True)  108 us
    all_to_all x1, waiting for transfers between devices, on_device(): lax.all_to_all(h, ('blk', 'shell'), split_axis=0, concat_axis=0, tiled=True)  50.6 us
    pallas_call x1, Pallas kernels, angular(): pl.pallas_call(angular_kernel, grid=(1024 // LT,), in_specs=[WHOLE, pl.Bl...  11.4 us
    all_to_all x1, starting transfers between devices, on_device(): lax.all_to_all(h, ('blk', 'shell'), split_axis=0, concat_axis=0, tiled=True)  8.91 us
    pallas_call x1, Pallas kernels, weigh(): pl.pallas_call(weigh_kernel, grid=(8,), in_specs=[pl.BlockSpec((1, 64), l...  8.65 us
    pallas_call x1, Pallas kernels, radial(): pl.pallas_call(radial_kernel, grid=(4,), in_specs=[WHOLE, pl.BlockSpec((1...  7.06 us
  transfers between devices with their start and end apart: 1, of which 1 were waited for; matrix products, arithmetic and copies ran while one was open for 0% of the time, Pallas kernels for 1%

profile of v2, /device:TPU:1, one launch (start us, length us, event | category | flops | bytes accessed | tf_op | source)
XLA Modules:
  0.0 199.9 jit_solution(8061585175956877921)
XLA Ops:
  0.0 1.4 reshape.22.sel_ref
  1.4 8.7 %weigh.1 = bf16[128,8,16,128]{3,2,1,0:T(8,128)(2,1)} custom-call(s32[1,64]{1,0:T(1,128)} %bitcast.13, f32[16,128]{1,0:T(8,128)} %reshape.22.sel_ref, bf16[8,2048,128]{2,1,0:T(8,128)(2,1)} %bitcast.10), custom_call_target="tpu_custom_call" | custom-call | flops 536870912 | bytes 8388608 | tf_op jit(solution)/shard_map/weigh/pallas_call | solution.py:42
  10.0 108.2 %all_to_all.10.r_ref = bf16[32,512,128]{2,1,0:T(8,128)(2,1)} all-to-all(bf16[32,512,128]{2,1,0:T(8,128)(2,1)} %bitcast.8), channel_id=1, replica_groups=mesh['blk'=32,'shell'=8] {'blk'}, dimensions={0} | all-to-all | bytes 8388608 | tf_op jit(solution)/shard_map/all_to_all | solution.py:162
  118.2 11.4 %angular.1 = bf16[8192,128]{1,0:T(8,128)(2,1)} custom-call(bf16[32,512,128]{2,1,0:T(8,128)(2,1)} %all_to_all.10.r_ref, bf16[2,2048,1024]{2,1,0:T(8,128)(2,1)} %leg_ref.1), custom_call_target="tpu_custom_call" | custom-call | flops 4294967296 | bytes 14680064 | tf_op jit(solution)/shard_map/angular/pallas_call | solution.py:92
  129.6 8.9 %all-to-all-start.1 = ((bf16[256,32,128]{2,1,0:T(8,128)(2,1)}), bf16[256,32,128]{2,1,0:T(8,128)(2,1)S(1)}, u32[]{:S(2)}, u32[]{:S(2)}) async-start(bf16[256,32,128]{2,1,0:T(8,128)(2,1)} %bitcast.11), calls=%async_computation.1 | async-start | bytes 4194304 | tf_op jit(solution)/shard_map/all_to_all | solution.py:165
  138.5 2.4 %spread.1.wide_ref = bf16[512,1024]{1,0:T(8,128)(2,1)} custom-call(bf16[512,256]{1,0:T(8,128)(2,1)} %bitcast.12), custom_call_target="tpu_custom_call" | custom-call | flops 268435456 | bytes 2097152 | tf_op jit(solution)/shard_map/spread/pallas_call | solution.py:113
  140.9 50.6 %all-to-all-done.1 = bf16[256,32,128]{2,1,0:T(8,128)(2,1)S(1)} async-done(((bf16[256,32,128]{2,1,0:T(8,128)(2,1)}), bf16[256,32,128]{2,1,0:T(8,128)(2,1)S(1)}, u32[]{:S(2)}, u32[]{:S(2)}) %all-to-all-start.1) | async-done | bytes 2097184 | tf_op jit(solution)/shard_map/all_to_all | solution.py:165
  191.5 0.0 copy-start
  191.5 1.3 copy-done
  192.9 7.1 %radial.1 = f32[4,8,128,128]{3,2,1,0:T(8,128)} custom-call(bf16[8192,128]{1,0:T(8,128)(2,1)} %bitcast.9, bf16[512,1024]{1,0:T(8,128)(2,1)} %spread.1.wide_ref), custom_call_target="tpu_custom_call" | custom-call | flops 1073741824 | bytes 5242880 | tf_op jit(solution)/shard_map/radial/pallas_call | solution.py:147
Async XLA Ops:
  129.6 61.9 %all-to-all-start.1 = ((bf16[256,32,128]{2,1,0:T(8,128)(2,1)}), bf16[256,32,128]{2,1,0:T(8,128)(2,1)S(1)}, u32[]{:S(2)}, u32[]{:S(2)}) async-start(bf16[256,32,128]{2,1,0:T(8,128)(2,1)} %bitcast.11), calls=%async_computation.1 | async-start | bytes 4194304 | tf_op jit(solution)/shard_map/all_to_all | solution.py:165
  191.5 1.3 copy-start

commit v3 on v2

--- a/solution.py
+++ b/solution.py
@@ -17,10 +17,18 @@
     return pl.CostEstimate(flops=flops, bytes_accessed=moved, transcendentals=0)
 
 
+RAWSEL = True
 PITCH = 16
 
 
-def weigh_kernel(perm_ref, sel_ref, x_ref, o_ref, scr):
+def weigh_kernel(perm_ref, sel_ref, x_ref, o_ref, scr, pair):
+    @pl.when(pl.program_id(0) == 0)
+    def _():
+        for rp in range(16):
+            pair[rp : rp + 1, :] = jnp.concatenate(
+                [sel_ref[2 * rp : 2 * rp + 1, :], sel_ref[2 * rp + 1 : 2 * rp + 2, :]], axis=1
+            )
+
     p = lax.broadcasted_iota(jnp.int32, (128, 64), 0)
     lane = lax.broadcasted_iota(jnp.int32, (128, 64), 1)
     held = jnp.sum(jnp.where(p // 2 == lane, 2 * perm_ref[...] + p % 2, 0), axis=1, keepdims=True)
@@ -30,7 +38,7 @@
         y = lax.dot_general(pick, x_ref[0, g * 256 : (g + 1) * 256, :], NT, preferred_element_type=F32)
         for h in range(2):
             rp = 2 * g + h
-            scr[pl.ds(rp, 128, stride=PITCH), :] = y[:, h * 128 : (h + 1) * 128] * sel_ref[rp : rp + 1, :]
+            scr[pl.ds(rp, 128, stride=PITCH), :] = y[:, h * 128 : (h + 1) * 128] * pair[rp : rp + 1, :]
     if PITCH == 16:
         o_ref[:, 0, :, :] = scr[...].reshape(128, 16, 128).astype(BF)
     else:
@@ -44,13 +52,14 @@
         grid=(8,),
         in_specs=[
             pl.BlockSpec((1, 64), lambda i: (0, 0)),
-            pl.BlockSpec((16, 128), lambda i: (0, 0)),
+            pl.BlockSpec((32, 64), lambda i: (0, 0)),
             pl.BlockSpec((1, 2048, 128), lambda i: (i, 0, 0)),
         ],
         out_specs=pl.BlockSpec((128, 1, 16, 128), lambda i: (0, i, 0, 0)),
         out_shape=jax.ShapeDtypeStruct((128, 8, 16, 128), BF),
-        scratch_shapes=[pltpu.VMEM((128 * PITCH, 128), F32)],
+        scratch_shapes=[pltpu.VMEM((128 * PITCH, 128), F32), pltpu.VMEM((16, 128), F32)],
         name="weigh",
+        compiler_params=pltpu.CompilerParams(vmem_limit_bytes=8 << 20),
         cost_estimate=cost(2 * 16384 * 128 * 128, 8 << 20),
     )(perm, sel, x)
 
@@ -75,7 +84,7 @@
                     lhs[s, to + 64 : to + 128, ks] = jnp.concatenate([a[:, 64:], b[:, 64:]], axis=1)
 
     for s in range(2):
-        h = lax.dot_general(lhs[s], leg_ref[s], NN, preferred_element_type=F32)
+        h = lax.dot_general(lhs[s], leg_ref[s, :, pl.ds(pl.multiple_of(pl.program_id(0) * LT, LT), LT)], NN, preferred_element_type=F32)
         ht = h.T
         for n in range(4):
             scr[pl.ds(4 * s + n, LT, stride=LP), :] = ht[:, n * 128 : (n + 1) * 128]
@@ -92,11 +101,12 @@
     return pl.pallas_call(
         angular_kernel,
         grid=(1024 // LT,),
-        in_specs=[WHOLE, pl.BlockSpec((2, 2048, LT), lambda i: (0, 0, i))],
+        in_specs=[WHOLE, WHOLE],
         out_specs=pl.BlockSpec((LT * 8, 128), lambda i: (i, 0)),
-        out_shape=jax.ShapeDtypeStruct((8192, 128), BF),
+        out_shape=pltpu.HBM((8192, 128), BF),
         scratch_shapes=[pltpu.VMEM((2, 512, 2048), BF), pltpu.VMEM((LT * LP, 128), F32)],
         name="angular",
+        compiler_params=pltpu.CompilerParams(vmem_limit_bytes=24 << 20),
         cost_estimate=cost(2 * 1024 * 2048 * 1024, 14 << 20),
     )(r, leg)
 
@@ -116,6 +126,7 @@
         out_specs=WHOLE,
         out_shape=jax.ShapeDtypeStruct((512, 1024), BF),
         name="spread",
+        compiler_params=pltpu.CompilerParams(vmem_limit_bytes=8 << 20),
         cost_estimate=cost(2 * 512 * 256 * 1024, 2 << 20),
     )(bes)
 
@@ -152,13 +163,15 @@
         out_shape=jax.ShapeDtypeStruct((4, 8, 128, 128), F32),
         scratch_shapes=[pltpu.VMEM((8192, 128), F32), pltpu.VMEM((512, 1024), BF), pltpu.VMEM((256, 1024), BF)],
         name="radial",
+        compiler_params=pltpu.CompilerParams(vmem_limit_bytes=20 << 20),
         cost_estimate=cost(2 * 4 * 256 * 1024 * 512, 5 << 20),
     )(r, wide)
 
 
 def on_device(spectra, selection, legendre, bessel, order_perm):
     x = jnp.transpose(spectra, (1, 2, 3, 0)).reshape(8, 2048, 128)
-    w = weigh(order_perm.reshape(1, 64), selection.reshape(16, 128), x).reshape(32, 512, 128)
+    x = pltpu.with_memory_space_constraint(x, pltpu.HBM)
+    w = weigh(pltpu.with_memory_space_constraint(order_perm.reshape(1, 64), pltpu.HBM), pltpu.with_memory_space_constraint(selection, pltpu.HBM), x).reshape(32, 512, 128)
     w = lax.all_to_all(w, "blk", split_axis=0, concat_axis=0, tiled=True)
     wide = spread(bessel.reshape(512, 256))
     h = angular(w, legendre).reshape(256, 32, 128)

time: 201 us -> 192 us (0.955)
  Pallas kernels: 29.5 us -> 21.8 us
  local copies, waits for them, and re-layouts: 2.72 us -> 0.01 us
    pallas_call x1, Pallas kernels: 11.4 us -> 8.36 us  [angular(): pl.pallas_call(angular_kernel, grid=(1024 // LT,), in_specs=[WHOLE, WHOLE...]
  transfers between devices with their start and end apart: 1 -> 1, of which waited for: 1 -> 1; matrix products, arithmetic and copies ran while one was open for 0% -> 0% of each run, Pallas kernels for 1% -> 0%
where the time goes in v3:
time: 192 us; the launch traced here: 191 us
  blocking collectives  108 us (56%)
  waiting for transfers between devices  52.6 us (27%)
  Pallas kernels  21.8 us (11%)
  starting transfers between devices  8.92 us (5%)
    all_to_all x1, blocking collectives, on_device(): w = lax.all_to_all(w, 'blk', split_axis=0, concat_axis=0, tiled=True)  108 us
    all_to_all x1, waiting for transfers between devices, on_device(): lax.all_to_all(h, ('blk', 'shell'), split_axis=0, concat_axis=0, tiled=True)  52.6 us
    all_to_all x1, starting transfers between devices, on_device(): lax.all_to_all(h, ('blk', 'shell'), split_axis=0, concat_axis=0, tiled=True)  8.92 us
    pallas_call x1, Pallas kernels, angular(): pl.pallas_call(angular_kernel, grid=(1024 // LT,), in_specs=[WHOLE, WHOLE...  8.36 us
    pallas_call x1, Pallas kernels, weigh(): pl.pallas_call(weigh_kernel, grid=(8,), in_specs=[pl.BlockSpec((1, 64), l...  7.64 us
    pallas_call x1, Pallas kernels, radial(): pl.pallas_call(radial_kernel, grid=(4,), in_specs=[WHOLE, pl.BlockSpec((1...  5.31 us
  transfers between devices with their start and end apart: 1, of which 1 were waited for; matrix products, arithmetic and copies ran while one was open for 0% of the time, Pallas kernels for 0%

profile of v3, /device:TPU:1, one launch (start us, length us, event | category | flops | bytes accessed | tf_op | source)
XLA Modules:
  0.0 191.4 jit_solution(11322367421692972752)
XLA Ops:
  0.0 7.6 %weigh.1 = bf16[128,8,16,128]{3,2,1,0:T(8,128)(2,1)S(1)} custom-call(s32[1,64]{1,0:T(1,128)} %bitcast.13, f32[32,64]{1,0:T(8,128)} %sel_ref.1, bf16[8,2048,128]{2,1,0:T(8,128)(2,1)} %bitcast.11), custom_call_target="tpu_custom_call" | custom-call | flops 536870912 | bytes 8388608 | tf_op jit(solution)/shard_map/weigh/pallas_call | solution.py:50
  7.6 0.0 copy-start.1
  7.7 108.1 %all_to_all.10.r_ref = bf16[32,512,128]{2,1,0:T(8,128)(2,1)S(1)} all-to-all(bf16[32,512,128]{2,1,0:T(8,128)(2,1)S(1)} %bitcast.8), channel_id=1, replica_groups=mesh['blk'=32,'shell'=8] {'blk'}, dimensions={0} | all-to-all | bytes 8388608 | tf_op jit(solution)/shard_map/all_to_all | solution.py:175
  115.8 0.0 copy-done.1
  115.8 8.4 %angular.1 = bf16[8192,128]{1,0:T(8,128)(2,1)} custom-call(bf16[32,512,128]{2,1,0:T(8,128)(2,1)S(1)} %all_to_all.10.r_ref, bf16[2,2048,1024]{2,1,0:T(8,128)(2,1)S(1)} %copy-done.1), custom_call_target="tpu_custom_call" | custom-call | flops 4294967296 | bytes 14680064 | tf_op jit(solution)/shard_map/angular/pallas_call | solution.py:101
  124.1 0.0 copy-start
  124.1 8.9 %all-to-all-start.1 = ((bf16[256,32,128]{2,1,0:T(8,128)(2,1)}), bf16[256,32,128]{2,1,0:T(8,128)(2,1)S(1)}, u32[]{:S(2)}, u32[]{:S(2)}) async-start(bf16[256,32,128]{2,1,0:T(8,128)(2,1)} %bitcast.12), calls=%async_computation.1 | async-start | bytes 4194304 | tf_op jit(solution)/shard_map/all_to_all | solution.py:178
  133.1 0.0 copy-done
  133.1 0.5 spread.1.wide_ref
  133.5 52.6 %all-to-all-done.1 = bf16[256,32,128]{2,1,0:T(8,128)(2,1)S(1)} async-done(((bf16[256,32,128]{2,1,0:T(8,128)(2,1)}), bf16[256,32,128]{2,1,0:T(8,128)(2,1)S(1)}, u32[]{:S(2)}, u32[]{:S(2)}) %all-to-all-start.1) | async-done | bytes 2097184 | tf_op jit(solution)/shard_map/all_to_all | solution.py:178
  186.1 5.3 %radial.1 = f32[4,8,128,128]{3,2,1,0:T(8,128)} custom-call(bf16[8192,128]{1,0:T(8,128)(2,1)S(1)} %bitcast.9, bf16[512,1024]{1,0:T(8,128)(2,1)S(1)} %spread.1.wide_ref), custom_call_target="tpu_custom_call" | custom-call | flops 1073741824 | bytes 5242880 | tf_op jit(solution)/shard_map/radial/pallas_call | solution.py:158
Async XLA Ops:
  7.6 108.1 %copy-start.1 = (bf16[2,2048,1024]{2,1,0:T(8,128)(2,1)S(1)}, bf16[2,2048,1024]{2,1,0:T(8,128)(2,1)}, u32[]{:S(2)}) copy-start(bf16[2,2048,1024]{2,1,0:T(8,128)(2,1)} %leg_ref.1) | copy-start | bytes 25165828
  124.1 8.9 %copy-start = (bf16[4,128,256]{2,1,0:T(8,128)(2,1)S(1)}, bf16[4,128,256]{2,1,0:T(8,128)(2,1)}, u32[]{:S(2)}) copy-start(bf16[4,128,256]{2,1,0:T(8,128)(2,1)} %param.8) | copy-start | bytes 786436
  124.1 61.9 %all-to-all-start.1 = ((bf16[256,32,128]{2,1,0:T(8,128)(2,1)}), bf16[256,32,128]{2,1,0:T(8,128)(2,1)S(1)}, u32[]{:S(2)}, u32[]{:S(2)}) async-start(bf16[256,32,128]{2,1,0:T(8,128)(2,1)} %bitcast.12), calls=%async_computation.1 | async-start | bytes 4194304 | tf_op jit(solution)/shard_map/all_to_all | solution.py:178

commit v4 on v3

--- a/solution.py
+++ b/solution.py
@@ -17,55 +17,72 @@
     return pl.CostEstimate(flops=flops, bytes_accessed=moved, transcendentals=0)
 
 
-RAWSEL = True
-PITCH = 16
-
-
-def weigh_kernel(perm_ref, sel_ref, x_ref, o_ref, scr, pair):
+FS = 4
+
+
+def onehot(rows, where):
+    row = lax.broadcasted_iota(jnp.int32, (rows, rows), 0)
+    col = lax.broadcasted_iota(jnp.int32, (rows, rows), 1)
+    return jnp.where(where(row) == col, 1.0, 0.0).astype(BF)
+
+
+def weigh_kernel(perm_ref, sel_ref, x_ref, o_ref, pair, pick_ref, swap):
     @pl.when(pl.program_id(0) == 0)
     def _():
         for rp in range(16):
-            pair[rp : rp + 1, :] = jnp.concatenate(
+            pair[:, rp * 128 : (rp + 1) * 128] = jnp.concatenate(
                 [sel_ref[2 * rp : 2 * rp + 1, :], sel_ref[2 * rp + 1 : 2 * rp + 2, :]], axis=1
             )
-
-    p = lax.broadcasted_iota(jnp.int32, (128, 64), 0)
-    lane = lax.broadcasted_iota(jnp.int32, (128, 64), 1)
-    held = jnp.sum(jnp.where(p // 2 == lane, 2 * perm_ref[...] + p % 2, 0), axis=1, keepdims=True)
-    col = lax.broadcasted_iota(jnp.int32, (128, 128), 1)
-    pick = jnp.where(held == col, 1.0, 0.0).astype(BF)
-    for g in range(8):
-        y = lax.dot_general(pick, x_ref[0, g * 256 : (g + 1) * 256, :], NT, preferred_element_type=F32)
-        for h in range(2):
-            rp = 2 * g + h
-            scr[pl.ds(rp, 128, stride=PITCH), :] = y[:, h * 128 : (h + 1) * 128] * pair[rp : rp + 1, :]
-    if PITCH == 16:
-        o_ref[:, 0, :, :] = scr[...].reshape(128, 16, 128).astype(BF)
-    else:
-        for q in range(128):
-            o_ref[q, 0, :, :] = scr[q * PITCH : q * PITCH + 16, :].astype(BF)
+        p = lax.broadcasted_iota(jnp.int32, (128, 64), 0)
+        lane = lax.broadcasted_iota(jnp.int32, (128, 64), 1)
+        held = jnp.sum(jnp.where(p // 2 == lane, 2 * perm_ref[...] + p % 2, 0), axis=1, keepdims=True)
+        col = lax.broadcasted_iota(jnp.int32, (128, 128), 1)
+        pick_ref[...] = jnp.where(held == col, 1.0, 0.0).astype(BF)
+        swap[...] = onehot(256, lambda i: i % 16 * 16 + i // 16)
+
+    for t in range(FS):
+        f = pl.program_id(0) * FS + t
+        ws = []
+        for g in range(8):
+            y = lax.dot_general(
+                pick_ref[...], x_ref[t, g * 256 : (g + 1) * 256, :], NT, preferred_element_type=F32
+            )
+            ws.append((y * pair[:, g * 256 : (g + 1) * 256]).astype(BF))
+        for k in range(0, 8, 2):
+            rows = jnp.concatenate(
+                [
+                    jnp.concatenate(
+                        [ws[rp // 2][(k + h) * 16 : (k + h + 1) * 16, rp % 2 * 128 : rp % 2 * 128 + 128] for h in range(2)],
+                        axis=1,
+                    )
+                    for rp in range(16)
+                ],
+                axis=0,
+            )
+            out = lax.dot_general(swap[...], rows, NN, preferred_element_type=F32).astype(BF)
+            for h in range(2):
+                o_ref[(k + h) * 16 : (k + h + 1) * 16, f, :, :] = out[:, h * 128 : (h + 1) * 128].reshape(16, 16, 128)
 
 
 def weigh(perm, sel, x):
     return pl.pallas_call(
         weigh_kernel,
-        grid=(8,),
+        grid=(8 // FS,),
         in_specs=[
             pl.BlockSpec((1, 64), lambda i: (0, 0)),
             pl.BlockSpec((32, 64), lambda i: (0, 0)),
-            pl.BlockSpec((1, 2048, 128), lambda i: (i, 0, 0)),
+            pl.BlockSpec((FS, 2048, 128), lambda i: (i, 0, 0)),
         ],
-        out_specs=pl.BlockSpec((128, 1, 16, 128), lambda i: (0, i, 0, 0)),
+        out_specs=WHOLE,
         out_shape=jax.ShapeDtypeStruct((128, 8, 16, 128), BF),
-        scratch_shapes=[pltpu.VMEM((128 * PITCH, 128), F32), pltpu.VMEM((16, 128), F32)],
+        scratch_shapes=[pltpu.VMEM((1, 2048), F32), pltpu.VMEM((128, 128), BF), pltpu.VMEM((256, 256), BF)],
         name="weigh",
-        compiler_params=pltpu.CompilerParams(vmem_limit_bytes=8 << 20),
+        compiler_params=pltpu.CompilerParams(vmem_limit_bytes=20 << 20),
         cost_estimate=cost(2 * 16384 * 128 * 128, 8 << 20),
     )(perm, sel, x)
 
 
-LT = 256
-LP = 8
+LT = 1024
 
 
 def angular_kernel(r_ref, leg_ref, o_ref, lhs, scr):
@@ -87,14 +104,8 @@
         h = lax.dot_general(lhs[s], leg_ref[s, :, pl.ds(pl.multiple_of(pl.program_id(0) * LT, LT), LT)], NN, preferred_element_type=F32)
         ht = h.T
         for n in range(4):
-            scr[pl.ds(4 * s + n, LT, stride=LP), :] = ht[:, n * 128 : (n + 1) * 128]
-    if LP == 8:
-        o_ref[...] = scr[...].astype(BF)
-    else:
-        for l in range(0, LT, 2):
-            o_ref[l * 8 : l * 8 + 16, :] = jnp.concatenate(
-                [scr[l * LP : l * LP + 8, :], scr[(l + 1) * LP : (l + 1) * LP + 8, :]], axis=0
-            ).astype(BF)
+            scr[pl.ds(4 * s + n, LT, stride=8), :] = ht[:, n * 128 : (n + 1) * 128]
+    o_ref[...] = scr[...].astype(BF)
 
 
 def angular(r, leg):
@@ -104,7 +115,7 @@
         in_specs=[WHOLE, WHOLE],
         out_specs=pl.BlockSpec((LT * 8, 128), lambda i: (i, 0)),
         out_shape=pltpu.HBM((8192, 128), BF),
-        scratch_shapes=[pltpu.VMEM((2, 512, 2048), BF), pltpu.VMEM((LT * LP, 128), F32)],
+        scratch_shapes=[pltpu.VMEM((2, 512, 2048), BF), pltpu.VMEM((LT * 8, 128), F32)],
         name="angular",
         compiler_params=pltpu.CompilerParams(vmem_limit_bytes=24 << 20),
         cost_estimate=cost(2 * 1024 * 2048 * 1024, 14 << 20),
@@ -131,27 +142,36 @@
     )(bes)
 
 
-def radial_kernel(r_ref, wide_ref, o_ref, f32s, weight, held):
+def radial_kernel(r_ref, wide_ref, o_ref, held, weight):
     l = pl.program_id(0)
 
     @pl.when(l == 0)
     def _():
-        f32s[...] = r_ref[...].astype(F32)
+        swap = onehot(128, lambda i: i % 16 // 4 * 32 + i // 16 % 4 * 8 + i % 4 * 2 + i // 64)
+        for g in range(8):
+            rows = jnp.concatenate(
+                [
+                    jnp.concatenate(
+                        [r_ref[(b * 8 + q) * 32 : (b * 8 + q) * 32 + 32, :] for b in range(g * 4, g * 4 + 4)], axis=0
+                    )
+                    for q in range(8)
+                ],
+                axis=1,
+            )
+            out = lax.dot_general(swap, rows, NN, preferred_element_type=F32).astype(BF)
+            for fh in range(2):
+                for n in range(4):
+                    at = (fh * 4 + n) * 16
+                    held[n, fh * 128 + g * 16 : fh * 128 + g * 16 + 16, :] = out[at : at + 16, :]
 
     field = (lax.broadcasted_iota(jnp.int32, (128, 1024), 1) // 16) % 4
     tiled = wide_ref[...]
     for f in range(4):
         weight[f * 128 : (f + 1) * 128, :] = jnp.where(field == f, tiled, jnp.zeros_like(tiled))
-    for n in range(8):
-        for q in range(8):
-            held[n * 32 : (n + 1) * 32, q * 128 : (q + 1) * 128] = f32s[
-                pl.ds(q * 32 + l * 8 + n, 32, stride=256), :
-            ].astype(BF)
-    y = lax.dot_general(held[...], weight[...], NT, preferred_element_type=F32)
-    for n in range(8):
-        p, fh = n // 2, n % 2
+    y = lax.dot_general(held[l], weight[...], NT, preferred_element_type=F32)
+    for fh in range(2):
         for f in range(4):
-            o_ref[0, fh * 4 + f, pl.ds(p, 32, stride=4), :] = y[n * 32 : (n + 1) * 32, f * 128 : (f + 1) * 128]
+            o_ref[0, fh * 4 + f, :, :] = y[fh * 128 : (fh + 1) * 128, f * 128 : (f + 1) * 128]
 
 
 def radial(r, wide):
@@ -161,7 +181,7 @@
         in_specs=[WHOLE, pl.BlockSpec((128, 1024), lambda i: (i, 0))],
         out_specs=pl.BlockSpec((1, 8, 128, 128), lambda i: (i, 0, 0, 0)),
         out_shape=jax.ShapeDtypeStruct((4, 8, 128, 128), F32),
-        scratch_shapes=[pltpu.VMEM((8192, 128), F32), pltpu.VMEM((512, 1024), BF), pltpu.VMEM((256, 1024), BF)],
+        scratch_shapes=[pltpu.VMEM((4, 256, 1024), BF), pltpu.VMEM((512, 1024), BF)],
         name="radial",
         compiler_params=pltpu.CompilerParams(vmem_limit_bytes=20 << 20),
         cost_estimate=cost(2 * 4 * 256 * 1024 * 512, 5 << 20),

time: 192 us -> 186 us (0.969)
  Pallas kernels: 21.8 us -> 16 us
    pallas_call x1, Pallas kernels: 7.64 us -> 5.27 us  [weigh(): pl.pallas_call(weigh_kernel, grid=(8 // FS,), in_specs=[pl.BlockSpec((1,...]
where the time goes in v4:
time: 186 us
  blocking collectives  108 us (58%)
  waiting for transfers between devices  52.6 us (28%)
  Pallas kernels  16 us (9%)
  starting transfers between devices  8.92 us (5%)
    all_to_all x1, blocking collectives, on_device(): w = lax.all_to_all(w, 'blk', split_axis=0, concat_axis=0, tiled=True)  108 us
    all_to_all x1, waiting for transfers between devices, on_device(): lax.all_to_all(h, ('blk', 'shell'), split_axis=0, concat_axis=0, tiled=True)  52.6 us
    all_to_all x1, starting transfers between devices, on_device(): lax.all_to_all(h, ('blk', 'shell'), split_axis=0, concat_axis=0, tiled=True)  8.92 us
    pallas_call x1, Pallas kernels, angular(): pl.pallas_call(angular_kernel, grid=(1024 // LT,), in_specs=[WHOLE, WHOLE...  6.5 us
    pallas_call x1, Pallas kernels, weigh(): pl.pallas_call(weigh_kernel, grid=(8 // FS,), in_specs=[pl.BlockSpec((1,...  5.27 us
    pallas_call x1, Pallas kernels, radial(): pl.pallas_call(radial_kernel, grid=(4,), in_specs=[WHOLE, pl.BlockSpec((1...  3.74 us
  transfers between devices with their start and end apart: 1, of which 1 were waited for; matrix products, arithmetic and copies ran while one was open for 0% of the time, Pallas kernels for 0%

profile of v4, /device:TPU:1, one launch (start us, length us, event | category | flops | bytes accessed | tf_op | source)
XLA Modules:
  0.0 185.6 jit_solution(15443437633894569416)
XLA Ops:
  0.0 5.3 %weigh.1 = bf16[128,8,16,128]{3,2,1,0:T(8,128)(2,1)S(1)} custom-call(s32[1,64]{1,0:T(1,128)} %bitcast.13, f32[32,64]{1,0:T(8,128)} %sel_ref.1, bf16[8,2048,128]{2,1,0:T(8,128)(2,1)} %bitcast.11), custom_call_target="tpu_custom_call" | custom-call | flops 536870912 | bytes 8388608 | tf_op jit(solution)/shard_map/weigh/pallas_call | solution.py:68
  5.3 0.0 copy-start.1
  5.3 108.1 %all_to_all.10.r_ref = bf16[32,512,128]{2,1,0:T(8,128)(2,1)S(1)} all-to-all(bf16[32,512,128]{2,1,0:T(8,128)(2,1)S(1)} %bitcast.8), channel_id=1, replica_groups=mesh['blk'=32,'shell'=8] {'blk'}, dimensions={0} | all-to-all | bytes 8388608 | tf_op jit(solution)/shard_map/all_to_all | solution.py:195
  113.4 0.0 copy-done.1
  113.4 6.5 %angular.1 = bf16[8192,128]{1,0:T(8,128)(2,1)} custom-call(bf16[32,512,128]{2,1,0:T(8,128)(2,1)S(1)} %all_to_all.10.r_ref, bf16[2,2048,1024]{2,1,0:T(8,128)(2,1)S(1)} %copy-done.1), custom_call_target="tpu_custom_call" | custom-call | flops 4294967296 | bytes 14680064 | tf_op jit(solution)/shard_map/angular/pallas_call | solution.py:112
  119.9 0.0 copy-start
  119.9 8.9 %all-to-all-start.1 = ((bf16[256,32,128]{2,1,0:T(8,128)(2,1)}), bf16[256,32,128]{2,1,0:T(8,128)(2,1)S(1)}, u32[]{:S(2)}, u32[]{:S(2)}) async-start(bf16[256,32,128]{2,1,0:T(8,128)(2,1)} %bitcast.12), calls=%async_computation.1 | async-start | bytes 4194304 | tf_op jit(solution)/shard_map/all_to_all | solution.py:198
  128.8 0.0 copy-done
  128.8 0.5 spread.1.wide_ref
  129.3 52.6 %all-to-all-done.1 = bf16[256,32,128]{2,1,0:T(8,128)(2,1)S(1)} async-done(((bf16[256,32,128]{2,1,0:T(8,128)(2,1)}), bf16[256,32,128]{2,1,0:T(8,128)(2,1)S(1)}, u32[]{:S(2)}, u32[]{:S(2)}) %all-to-all-start.1) | async-done | bytes 2097184 | tf_op jit(solution)/shard_map/all_to_all | solution.py:198
  181.9 3.7 %radial.1 = f32[4,8,128,128]{3,2,1,0:T(8,128)} custom-call(bf16[8192,128]{1,0:T(8,128)(2,1)S(1)} %bitcast.9, bf16[512,1024]{1,0:T(8,128)(2,1)S(1)} %spread.1.wide_ref), custom_call_target="tpu_custom_call" | custom-call | flops 1073741824 | bytes 5242880 | tf_op jit(solution)/shard_map/radial/pallas_call | solution.py:178
Async XLA Ops:
  5.3 108.1 %copy-start.1 = (bf16[2,2048,1024]{2,1,0:T(8,128)(2,1)S(1)}, bf16[2,2048,1024]{2,1,0:T(8,128)(2,1)}, u32[]{:S(2)}) copy-start(bf16[2,2048,1024]{2,1,0:T(8,128)(2,1)} %leg_ref.1) | copy-start | bytes 25165828
  119.9 8.9 %copy-start = (bf16[4,128,256]{2,1,0:T(8,128)(2,1)S(1)}, bf16[4,128,256]{2,1,0:T(8,128)(2,1)}, u32[]{:S(2)}) copy-start(bf16[4,128,256]{2,1,0:T(8,128)(2,1)} %param.8) | copy-start | bytes 786436
  119.9 62.0 %all-to-all-start.1 = ((bf16[256,32,128]{2,1,0:T(8,128)(2,1)}), bf16[256,32,128]{2,1,0:T(8,128)(2,1)S(1)}, u32[]{:S(2)}, u32[]{:S(2)}) async-start(bf16[256,32,128]{2,1,0:T(8,128)(2,1)} %bitcast.12), calls=%async_computation.1 | async-start | bytes 4194304 | tf_op jit(solution)/shard_map/all_to_all | solution.py:198

commit v5 on v4

--- a/solution.py
+++ b/solution.py
@@ -113,8 +113,8 @@
         angular_kernel,
         grid=(1024 // LT,),
         in_specs=[WHOLE, WHOLE],
-        out_specs=pl.BlockSpec((LT * 8, 128), lambda i: (i, 0)),
-        out_shape=pltpu.HBM((8192, 128), BF),
+        out_specs=WHOLE,
+        out_shape=jax.ShapeDtypeStruct((8192, 128), BF),
         scratch_shapes=[pltpu.VMEM((2, 512, 2048), BF), pltpu.VMEM((LT * 8, 128), F32)],
         name="angular",
         compiler_params=pltpu.CompilerParams(vmem_limit_bytes=24 << 20),
@@ -122,27 +122,7 @@
     )(r, leg)
 
 
-def spread_kernel(bes_ref, o_ref):
-    src = lax.broadcasted_iota(jnp.int32, (256, 1024), 0)
-    lam = lax.broadcasted_iota(jnp.int32, (256, 1024), 1)
-    shell = (lam // 128) * 32 + 2 * (lam % 16) + (lam // 64) % 2
-    one = jnp.where(src == shell, 1.0, 0.0).astype(BF)
-    o_ref[...] = lax.dot_general(bes_ref[...], one, NN, preferred_element_type=F32).astype(BF)
-
-
-def spread(bes):
-    return pl.pallas_call(
-        spread_kernel,
-        in_specs=[WHOLE],
-        out_specs=WHOLE,
-        out_shape=jax.ShapeDtypeStruct((512, 1024), BF),
-        name="spread",
-        compiler_params=pltpu.CompilerParams(vmem_limit_bytes=8 << 20),
-        cost_estimate=cost(2 * 512 * 256 * 1024, 2 << 20),
-    )(bes)
-
-
-def radial_kernel(r_ref, wide_ref, o_ref, held, weight):
+def radial_kernel(r_ref, bes_ref, o_ref, held, weight, spread):
     l = pl.program_id(0)
 
     @pl.when(l == 0)
@@ -164,8 +144,13 @@
                     at = (fh * 4 + n) * 16
                     held[n, fh * 128 + g * 16 : fh * 128 + g * 16 + 16, :] = out[at : at + 16, :]
 
+        src = lax.broadcasted_iota(jnp.int32, (256, 1024), 0)
+        lam = lax.broadcasted_iota(jnp.int32, (256, 1024), 1)
+        shell = (lam // 128) * 32 + 2 * (lam % 16) + (lam // 64) % 2
+        spread[...] = jnp.where(src == shell, 1.0, 0.0).astype(BF)
+
     field = (lax.broadcasted_iota(jnp.int32, (128, 1024), 1) // 16) % 4
-    tiled = wide_ref[...]
+    tiled = lax.dot_general(bes_ref[0], spread[...], NN, preferred_element_type=F32).astype(BF)
     for f in range(4):
         weight[f * 128 : (f + 1) * 128, :] = jnp.where(field == f, tiled, jnp.zeros_like(tiled))
     y = lax.dot_general(held[l], weight[...], NT, preferred_element_type=F32)
@@ -174,18 +159,18 @@
             o_ref[0, fh * 4 + f, :, :] = y[fh * 128 : (fh + 1) * 128, f * 128 : (f + 1) * 128]
 
 
-def radial(r, wide):
+def radial(r, bes):
     return pl.pallas_call(
         radial_kernel,
         grid=(4,),
-        in_specs=[WHOLE, pl.BlockSpec((128, 1024), lambda i: (i, 0))],
+        in_specs=[WHOLE, pl.BlockSpec((1, 128, 256), lambda i: (i, 0, 0))],
         out_specs=pl.BlockSpec((1, 8, 128, 128), lambda i: (i, 0, 0, 0)),
         out_shape=jax.ShapeDtypeStruct((4, 8, 128, 128), F32),
-        scratch_shapes=[pltpu.VMEM((4, 256, 1024), BF), pltpu.VMEM((512, 1024), BF)],
+        scratch_shapes=[pltpu.VMEM((4, 256, 1024), BF), pltpu.VMEM((512, 1024), BF), pltpu.VMEM((256, 1024), BF)],
         name="radial",
         compiler_params=pltpu.CompilerParams(vmem_limit_bytes=20 << 20),
         cost_estimate=cost(2 * 4 * 256 * 1024 * 512, 5 << 20),
-    )(r, wide)
+    )(r, bes)
 
 
 def on_device(spectra, selection, legendre, bessel, order_perm):
@@ -193,10 +178,9 @@
     x = pltpu.with_memory_space_constraint(x, pltpu.HBM)
     w = weigh(pltpu.with_memory_space_constraint(order_perm.reshape(1, 64), pltpu.HBM), pltpu.with_memory_space_constraint(selection, pltpu.HBM), x).reshape(32, 512, 128)
     w = lax.all_to_all(w, "blk", split_axis=0, concat_axis=0, tiled=True)
-    wide = spread(bessel.reshape(512, 256))
     h = angular(w, legendre).reshape(256, 32, 128)
     h = lax.all_to_all(h, ("blk", "shell"), split_axis=0, concat_axis=0, tiled=True)
-    return radial(h.reshape(8192, 128), wide)
+    return radial(h.reshape(8192, 128), bessel)
 
 
 def solution(mesh):

time: 186 us -> 185 us (level)
  blocking collectives: 108 us -> 170 us
  waiting for transfers between devices: 52.6 us -> 0 us
  starting transfers between devices: 8.92 us -> 0 us
    all_to_all x0 -> x1, blocking collectives: none -> 61.8 us  [on_device(): lax.all_to_all(h, ('blk', 'shell'), split_axis=0, concat_axis=0, tiled=True)]
    all_to_all x1 -> x0, waiting for transfers between devices: 52.6 us -> none  [on_device(): lax.all_to_all(h, ('blk', 'shell'), split_axis=0, concat_axis=0, tiled=True)]
    all_to_all x1 -> x0, starting transfers between devices: 8.92 us -> none  [on_device(): lax.all_to_all(h, ('blk', 'shell'), split_axis=0, concat_axis=0, tiled=True)]
  transfers between devices with their start and end apart: 1 -> 0, of which waited for: 1 -> 0; matrix products, arithmetic and copies ran while one was open for 0% -> 0% of each run, Pallas kernels for 0% -> 0%
where the time goes in v5:
time: 185 us
  blocking collectives  170 us (92%)
  Pallas kernels  14.8 us (8%)
    all_to_all x1, blocking collectives, on_device(): w = lax.all_to_all(w, 'blk', split_axis=0, concat_axis=0, tiled=True)  108 us
    all_to_all x1, blocking collectives, on_device(): lax.all_to_all(h, ('blk', 'shell'), split_axis=0, concat_axis=0, tiled=True)  61.8 us
    pallas_call x1, Pallas kernels, weigh(): pl.pallas_call(weigh_kernel, grid=(8 // FS,), in_specs=[pl.BlockSpec((1,...  5.27 us
    pallas_call x1, Pallas kernels, angular(): pl.pallas_call(angular_kernel, grid=(1024 // LT,), in_specs=[WHOLE, WHOLE...  5.18 us
    pallas_call x1, Pallas kernels, radial(): pl.pallas_call(radial_kernel, grid=(4,), in_specs=[WHOLE, pl.BlockSpec((1...  4.38 us

profile of v5, /device:TPU:1, one launch (start us, length us, event | category | flops | bytes accessed | tf_op | source)
XLA Modules:
  0.0 184.7 jit_solution(15660659195174476863)
XLA Ops:
  0.0 5.3 %weigh.1 = bf16[128,8,16,128]{3,2,1,0:T(8,128)(2,1)S(1)} custom-call(s32[1,64]{1,0:T(1,128)} %bitcast.11, f32[32,64]{1,0:T(8,128)} %sel_ref.1, bf16[8,2048,128]{2,1,0:T(8,128)(2,1)} %bitcast.10), custom_call_target="tpu_custom_call" | custom-call | flops 536870912 | bytes 8388608 | tf_op jit(solution)/shard_map/weigh/pallas_call | solution.py:68
  5.3 0.0 copy-start.1
  5.3 108.1 %all_to_all.10.r_ref = bf16[32,512,128]{2,1,0:T(8,128)(2,1)S(1)} all-to-all(bf16[32,512,128]{2,1,0:T(8,128)(2,1)S(1)} %bitcast.7), channel_id=1, replica_groups=mesh['blk'=32,'shell'=8] {'blk'}, dimensions={0} | all-to-all | bytes 8388608 | tf_op jit(solution)/shard_map/all_to_all | solution.py:180
  113.4 0.0 copy-done.1
  113.4 5.2 %angular.1 = bf16[8192,128]{1,0:T(8,128)(2,1)S(1)} custom-call(bf16[32,512,128]{2,1,0:T(8,128)(2,1)S(1)} %all_to_all.10.r_ref, bf16[2,2048,1024]{2,1,0:T(8,128)(2,1)S(1)} %copy-done.1), custom_call_target="tpu_custom_call" | custom-call | flops 4294967296 | bytes 14680064 | tf_op jit(solution)/shard_map/angular/pallas_call | solution.py:112
  118.6 0.0 copy-start
  118.6 61.8 %all_to_all.11 = bf16[256,32,128]{2,1,0:T(8,128)(2,1)S(1)} all-to-all(bf16[256,32,128]{2,1,0:T(8,128)(2,1)S(1)} %bitcast.9), channel_id=1, replica_groups=mesh['blk'=32,'shell'=8] {'blk','shell'}, dimensions={0} | all-to-all | bytes 4194304 | tf_op jit(solution)/shard_map/all_to_all | solution.py:182
  180.3 0.0 copy-done
  180.4 4.4 %radial.1 = f32[4,8,128,128]{3,2,1,0:T(8,128)} custom-call(bf16[8192,128]{1,0:T(8,128)(2,1)S(1)} %bitcast.8, bf16[4,128,256]{2,1,0:T(8,128)(2,1)S(1)} %copy-done), custom_call_target="tpu_custom_call" | custom-call | flops 1073741824 | bytes 5242880 | tf_op jit(solution)/shard_map/radial/pallas_call | solution.py:163
Async XLA Ops:
  5.3 108.1 %copy-start.1 = (bf16[2,2048,1024]{2,1,0:T(8,128)(2,1)S(1)}, bf16[2,2048,1024]{2,1,0:T(8,128)(2,1)}, u32[]{:S(2)}) copy-start(bf16[2,2048,1024]{2,1,0:T(8,128)(2,1)} %leg_ref.1) | copy-start | bytes 25165828
  118.6 61.8 %copy-start = (bf16[4,128,256]{2,1,0:T(8,128)(2,1)S(1)}, bf16[4,128,256]{2,1,0:T(8,128)(2,1)}, u32[]{:S(2)}) copy-start(bf16[4,128,256]{2,1,0:T(8,128)(2,1)} %bes_ref.1) | copy-start | bytes 786436

commit v6 on v5

--- a/solution.py
+++ b/solution.py
@@ -150,21 +150,22 @@
         spread[...] = jnp.where(src == shell, 1.0, 0.0).astype(BF)
 
     field = (lax.broadcasted_iota(jnp.int32, (128, 1024), 1) // 16) % 4
-    tiled = lax.dot_general(bes_ref[0], spread[...], NN, preferred_element_type=F32).astype(BF)
-    for f in range(4):
-        weight[f * 128 : (f + 1) * 128, :] = jnp.where(field == f, tiled, jnp.zeros_like(tiled))
-    y = lax.dot_general(held[l], weight[...], NT, preferred_element_type=F32)
-    for fh in range(2):
+    for t in range(2):
+        tiled = lax.dot_general(bes_ref[t], spread[...], NN, preferred_element_type=F32).astype(BF)
         for f in range(4):
-            o_ref[0, fh * 4 + f, :, :] = y[fh * 128 : (fh + 1) * 128, f * 128 : (f + 1) * 128]
+            weight[f * 128 : (f + 1) * 128, :] = jnp.where(field == f, tiled, jnp.zeros_like(tiled))
+        y = lax.dot_general(held[2 * l + t], weight[...], NT, preferred_element_type=F32)
+        for fh in range(2):
+            for f in range(4):
+                o_ref[t, fh * 4 + f, :, :] = y[fh * 128 : (fh + 1) * 128, f * 128 : (f + 1) * 128]
 
 
 def radial(r, bes):
     return pl.pallas_call(
         radial_kernel,
-        grid=(4,),
-        in_specs=[WHOLE, pl.BlockSpec((1, 128, 256), lambda i: (i, 0, 0))],
-        out_specs=pl.BlockSpec((1, 8, 128, 128), lambda i: (i, 0, 0, 0)),
+        grid=(2,),
+        in_specs=[WHOLE, pl.BlockSpec((2, 128, 256), lambda i: (i, 0, 0))],
+        out_specs=pl.BlockSpec((2, 8, 128, 128), lambda i: (i, 0, 0, 0)),
         out_shape=jax.ShapeDtypeStruct((4, 8, 128, 128), F32),
         scratch_shapes=[pltpu.VMEM((4, 256, 1024), BF), pltpu.VMEM((512, 1024), BF), pltpu.VMEM((256, 1024), BF)],
         name="radial",

time: 185 us -> 185 us (level)
  no operation moved by 1% of the time
where the time goes in v6:
time: 185 us; the launch traced here: 184 us
  blocking collectives  170 us (92%)
  Pallas kernels  14.5 us (8%)
    all_to_all x1, blocking collectives, on_device(): w = lax.all_to_all(w, 'blk', split_axis=0, concat_axis=0, tiled=True)  108 us
    all_to_all x1, blocking collectives, on_device(): lax.all_to_all(h, ('blk', 'shell'), split_axis=0, concat_axis=0, tiled=True)  61.8 us
    pallas_call x1, Pallas kernels, weigh(): pl.pallas_call(weigh_kernel, grid=(8 // FS,), in_specs=[pl.BlockSpec((1,...  5.27 us
    pallas_call x1, Pallas kernels, angular(): pl.pallas_call(angular_kernel, grid=(1024 // LT,), in_specs=[WHOLE, WHOLE...  5.18 us
    pallas_call x1, Pallas kernels, radial(): pl.pallas_call(radial_kernel, grid=(2,), in_specs=[WHOLE, pl.BlockSpec((2...  4.05 us

profile of v6, /device:TPU:1, one launch (start us, length us, event | category | flops | bytes accessed | tf_op | source)
XLA Modules:
  0.0 184.4 jit_solution(2441330822889214406)
XLA Ops:
  0.0 5.3 %weigh.1 = bf16[128,8,16,128]{3,2,1,0:T(8,128)(2,1)S(1)} custom-call(s32[1,64]{1,0:T(1,128)} %bitcast.11, f32[32,64]{1,0:T(8,128)} %sel_ref.1, bf16[8,2048,128]{2,1,0:T(8,128)(2,1)} %bitcast.10), custom_call_target="tpu_custom_call" | custom-call | flops 536870912 | bytes 8388608 | tf_op jit(solution)/shard_map/weigh/pallas_call | solution.py:68
  5.3 0.0 copy-start.1
  5.3 108.1 %all_to_all.10.r_ref = bf16[32,512,128]{2,1,0:T(8,128)(2,1)S(1)} all-to-all(bf16[32,512,128]{2,1,0:T(8,128)(2,1)S(1)} %bitcast.7), channel_id=1, replica_groups=mesh['blk'=32,'shell'=8] {'blk'}, dimensions={0} | all-to-all | bytes 8388608 | tf_op jit(solution)/shard_map/all_to_all | solution.py:181
  113.4 0.0 copy-done.1
  113.4 5.2 %angular.1 = bf16[8192,128]{1,0:T(8,128)(2,1)S(1)} custom-call(bf16[32,512,128]{2,1,0:T(8,128)(2,1)S(1)} %all_to_all.10.r_ref, bf16[2,2048,1024]{2,1,0:T(8,128)(2,1)S(1)} %copy-done.1), custom_call_target="tpu_custom_call" | custom-call | flops 4294967296 | bytes 14680064 | tf_op jit(solution)/shard_map/angular/pallas_call | solution.py:112
  118.6 0.0 copy-start
  118.6 61.8 %all_to_all.11 = bf16[256,32,128]{2,1,0:T(8,128)(2,1)S(1)} all-to-all(bf16[256,32,128]{2,1,0:T(8,128)(2,1)S(1)} %bitcast.9), channel_id=1, replica_groups=mesh['blk'=32,'shell'=8] {'blk','shell'}, dimensions={0} | all-to-all | bytes 4194304 | tf_op jit(solution)/shard_map/all_to_all | solution.py:183
  180.3 0.0 copy-done
  180.4 4.0 %radial.1 = f32[4,8,128,128]{3,2,1,0:T(8,128)} custom-call(bf16[8192,128]{1,0:T(8,128)(2,1)S(1)} %bitcast.8, bf16[4,128,256]{2,1,0:T(8,128)(2,1)S(1)} %copy-done), custom_call_target="tpu_custom_call" | custom-call | flops 1073741824 | bytes 5242880 | tf_op jit(solution)/shard_map/radial/pallas_call | solution.py:164
Async XLA Ops:
  5.3 108.1 %copy-start.1 = (bf16[2,2048,1024]{2,1,0:T(8,128)(2,1)S(1)}, bf16[2,2048,1024]{2,1,0:T(8,128)(2,1)}, u32[]{:S(2)}) copy-start(bf16[2,2048,1024]{2,1,0:T(8,128)(2,1)} %leg_ref.1) | copy-start | bytes 25165828
  118.6 61.8 %copy-start = (bf16[4,128,256]{2,1,0:T(8,128)(2,1)S(1)}, bf16[4,128,256]{2,1,0:T(8,128)(2,1)}, u32[]{:S(2)}) copy-start(bf16[4,128,256]{2,1,0:T(8,128)(2,1)} %bes_ref.1) | copy-start | bytes 786436

commit v7 on v6

--- a/solution.py
+++ b/solution.py
@@ -150,8 +150,10 @@
         spread[...] = jnp.where(src == shell, 1.0, 0.0).astype(BF)
 
     field = (lax.broadcasted_iota(jnp.int32, (128, 1024), 1) // 16) % 4
+    pair = bes_ref[...].reshape(256, 256)
+    both = lax.dot_general(pair, spread[...], NN, preferred_element_type=F32).astype(BF)
     for t in range(2):
-        tiled = lax.dot_general(bes_ref[t], spread[...], NN, preferred_element_type=F32).astype(BF)
+        tiled = both[t * 128 : (t + 1) * 128, :]
         for f in range(4):
             weight[f * 128 : (f + 1) * 128, :] = jnp.where(field == f, tiled, jnp.zeros_like(tiled))
         y = lax.dot_general(held[2 * l + t], weight[...], NT, preferred_element_type=F32)

time: 185 us -> 184 us (level)
  no operation moved by 1% of the time
where the time goes in v7:
time: 184 us
  blocking collectives  170 us (92%)
  Pallas kernels  14.1 us (8%)
    all_to_all x1, blocking collectives, on_device(): w = lax.all_to_all(w, 'blk', split_axis=0, concat_axis=0, tiled=True)  108 us
    all_to_all x1, blocking collectives, on_device(): lax.all_to_all(h, ('blk', 'shell'), split_axis=0, concat_axis=0, tiled=True)  61.8 us
    pallas_call x1, Pallas kernels, weigh(): pl.pallas_call(weigh_kernel, grid=(8 // FS,), in_specs=[pl.BlockSpec((1,...  5.27 us
    pallas_call x1, Pallas kernels, angular(): pl.pallas_call(angular_kernel, grid=(1024 // LT,), in_specs=[WHOLE, WHOLE...  5.18 us

profile of v7, /device:TPU:1, one launch (start us, length us, event | category | flops | bytes accessed | tf_op | source)
XLA Modules:
  0.0 184.0 jit_solution(18264360390181490232)
XLA Ops:
  0.0 5.3 %weigh.1 = bf16[128,8,16,128]{3,2,1,0:T(8,128)(2,1)S(1)} custom-call(s32[1,64]{1,0:T(1,128)} %bitcast.11, f32[32,64]{1,0:T(8,128)} %sel_ref.1, bf16[8,2048,128]{2,1,0:T(8,128)(2,1)} %bitcast.10), custom_call_target="tpu_custom_call" | custom-call | flops 536870912 | bytes 8388608 | tf_op jit(solution)/shard_map/weigh/pallas_call | solution.py:68
  5.3 0.0 copy-start.1
  5.3 108.1 %all_to_all.10.r_ref = bf16[32,512,128]{2,1,0:T(8,128)(2,1)S(1)} all-to-all(bf16[32,512,128]{2,1,0:T(8,128)(2,1)S(1)} %bitcast.7), channel_id=1, replica_groups=mesh['blk'=32,'shell'=8] {'blk'}, dimensions={0} | all-to-all | bytes 8388608 | tf_op jit(solution)/shard_map/all_to_all | solution.py:183
  113.4 0.0 copy-done.1
  113.4 5.2 %angular.1 = bf16[8192,128]{1,0:T(8,128)(2,1)S(1)} custom-call(bf16[32,512,128]{2,1,0:T(8,128)(2,1)S(1)} %all_to_all.10.r_ref, bf16[2,2048,1024]{2,1,0:T(8,128)(2,1)S(1)} %copy-done.1), custom_call_target="tpu_custom_call" | custom-call | flops 4294967296 | bytes 14680064 | tf_op jit(solution)/shard_map/angular/pallas_call | solution.py:112
  118.6 0.0 copy-start
  118.6 61.8 %all_to_all.11 = bf16[256,32,128]{2,1,0:T(8,128)(2,1)S(1)} all-to-all(bf16[256,32,128]{2,1,0:T(8,128)(2,1)S(1)} %bitcast.9), channel_id=1, replica_groups=mesh['blk'=32,'shell'=8] {'blk','shell'}, dimensions={0} | all-to-all | bytes 4194304 | tf_op jit(solution)/shard_map/all_to_all | solution.py:185
  180.3 0.0 copy-done
  180.4 3.7 %radial.1 = f32[4,8,128,128]{3,2,1,0:T(8,128)} custom-call(bf16[8192,128]{1,0:T(8,128)(2,1)S(1)} %bitcast.8, bf16[4,128,256]{2,1,0:T(8,128)(2,1)S(1)} %copy-done), custom_call_target="tpu_custom_call" | custom-call | flops 1073741824 | bytes 5242880 | tf_op jit(solution)/shard_map/radial/pallas_call | solution.py:166
Async XLA Ops:
  5.3 108.1 %copy-start.1 = (bf16[2,2048,1024]{2,1,0:T(8,128)(2,1)S(1)}, bf16[2,2048,1024]{2,1,0:T(8,128)(2,1)}, u32[]{:S(2)}) copy-start(bf16[2,2048,1024]{2,1,0:T(8,128)(2,1)} %leg_ref.1) | copy-start | bytes 25165828
  118.6 61.8 %copy-start = (bf16[4,128,256]{2,1,0:T(8,128)(2,1)S(1)}, bf16[4,128,256]{2,1,0:T(8,128)(2,1)}, u32[]{:S(2)}) copy-start(bf16[4,128,256]{2,1,0:T(8,128)(2,1)} %bes_ref.1) | copy-start | bytes 786436
